TPU v7x, 512 devices: a whole 4x8x8 slice. The times are simulated.
512 devices in a mesh: rows: 512 (over y, x, z, core).
Axes of the slice: x: 4, y: 8, z: 8, core: 2. Of those that a mesh axis runs over, the one named last changes fastest.
Arguments:
- rhs: float32 [131072, 512], P('rows'), may hold values from -6 to 6
- v_basis0: float32 [131072, 256], P('rows'), may hold values from -0.0234375 to 0.0234375
- w_basis0: float32 [131072, 256], P('rows'), may hold values from -0.375 to 0.375
- cap_inv0: float32 [512, 512], P('rows'), may hold values from -0.25 to 0.25
- v_basis1: float32 [131072, 256], P('rows'), may hold values from -0.03125 to 0.03125
- w_basis1: float32 [131072, 256], P('rows'), may hold values from -0.375 to 0.375
- cap_inv1: float32 [1024, 512], P('rows'), may hold values from -0.25 to 0.25
- v_basis2: float32 [131072, 256], P('rows'), may hold values from -0.046875 to 0.046875
- w_basis2: float32 [131072, 256], P('rows'), may hold values from -0.375 to 0.375
- cap_inv2: float32 [2048, 512], P('rows'), may hold values from -0.25 to 0.25
Outputs:
- solved: float32 [131072, 512], P('rows')
All inputs are finite; a program needn't handle non-finite values.
Results may differ from a plain program's by a relative error of at most 0.00014.
Values sent between devices are 32-bit elements; how exact they have to be, the bound alone decides.
A program may use at most 64 MiB of HBM per device.

v0:
```python
import jax
import jax.numpy as jnp
from jax import lax
from jax.sharding import PartitionSpec as P


def from_partner(block, axis, bit):
    count = lax.axis_size(axis)
    route = []
    for low in range(count):
        high = low | 1 << bit
        if high != low and high < count:
            route += [(low, high), (high, low)]
    return lax.ppermute(block, axis, route)


def group_total(partial_value, group_bits):
    for bit in range(group_bits):
        partial_value = partial_value + from_partner(partial_value, "rows", bit)
    return partial_value


def collect_coef(piece, group_bits, index):
    for bit in range(group_bits):
        other = from_partner(piece, "rows", bit)
        first = index >> bit & 1 == 0
        piece = jnp.where(
            first, jnp.concatenate([piece, other], axis=0), jnp.concatenate([other, piece], axis=0)
        )
    return piece


def apply_level(state, v_basis, w_basis, cap_inv, level, nbits, index):
    group_bits = nbits - level - 1
    side = index >> group_bits & 1
    partial_value = lax.dot_general(
        v_basis,
        state,
        (((0,), (0,)), ((), ())),
        precision=lax.Precision.HIGHEST,
        preferred_element_type=jnp.float32,
    )
    own = group_total(partial_value, group_bits)
    other = from_partner(own, "rows", group_bits)
    stacked = jnp.where(
        side == 0, jnp.concatenate([other, own], axis=0), jnp.concatenate([own, other], axis=0)
    )
    piece = jnp.dot(
        cap_inv, stacked, precision=lax.Precision.HIGHEST, preferred_element_type=jnp.float32
    )
    coef = collect_coef(piece, group_bits, index)
    update = jnp.dot(
        w_basis, coef, precision=lax.Precision.HIGHEST, preferred_element_type=jnp.float32
    )
    return state - update


def shards(
    rhs, v_basis0, w_basis0, cap_inv0, v_basis1, w_basis1, cap_inv1, v_basis2, w_basis2, cap_inv2
):
    nbits = lax.axis_size("rows").bit_length() - 1
    index = lax.axis_index("rows")
    state = apply_level(rhs, v_basis2, w_basis2, cap_inv2, 2, nbits, index)
    state = apply_level(state, v_basis1, w_basis1, cap_inv1, 1, nbits, index)
    state = apply_level(state, v_basis0, w_basis0, cap_inv0, 0, nbits, index)
    return state


def solution(mesh):
    in_specs = (
        P("rows", None),
        P("rows", None),
        P("rows", None),
        P("rows", None),
        P("rows", None),
        P("rows", None),
        P("rows", None),
        P("rows", None),
        P("rows", None),
        P("rows", None),
    )
    out_specs = P("rows", None)
    return jax.shard_map(shards, mesh=mesh, in_specs=in_specs, out_specs=out_specs, check_vma=False)
```

profile of v0, /device:TPU:1, one launch (start us, length us, event | category | flops | bytes accessed | tf_op | source)
XLA Modules:
  0.0 604.1 jit_solution(14040928936806059123)
XLA Ops:
  2.6 8.8 %collective-permute-start = (f32[256,512]{1,0:T(8,128)S(1)}, f32[256,512]{1,0:T(8,128)S(1)}, u32[]{:S(2)}, u32[]{:S(2)}) collective-permute-start(f32[256,512]{1,0:T(8,128)S(1)} %fusion.47), channel_id=1, source_target_pairs={{0,1},{1,0},{2,3},{3,2},{4,5},{5,4},{6,7},{7,6},{8,9},{9,8},{10,11... | collective-permute-start | bytes 1572872 | tf_op jit(solution)/shard_map/ppermute | solution.py:14
  14.9 13.1 %collective-permute-done.1 = f32[256,512]{1,0:T(8,128)S(1)} collective-permute-done((f32[256,512]{1,0:T(8,128)S(1)}, f32[256,512]{1,0:T(8,128)S(1)}, u32[]{:S(2)}, u32[]{:S(2)}) %collective-permute-start.1) | collective-permute-done | bytes 524320 | tf_op jit(solution)/shard_map/ppermute | solution.py:14
  30.1 25.9 %collective-permute-done.2 = f32[256,512]{1,0:T(8,128)S(1)} collective-permute-done((f32[256,512]{1,0:T(8,128)S(1)}, f32[256,512]{1,0:T(8,128)S(1)}, u32[]{:S(2)}, u32[]{:S(2)}) %collective-permute-start.2) | collective-permute-done | bytes 524320 | tf_op jit(solution)/shard_map/ppermute | solution.py:14
  56.0 4.3 collective-permute-start.3
  60.4 25.9 %collective-permute-done.3 = f32[256,512]{1,0:T(8,128)S(1)} collective-permute-done((f32[256,512]{1,0:T(8,128)S(1)}, f32[256,512]{1,0:T(8,128)S(1)}, u32[]{:S(2)}, u32[]{:S(2)}) %collective-permute-start.3) | collective-permute-done | bytes 524320 | tf_op jit(solution)/shard_map/ppermute | solution.py:14
  88.3 13.0 %collective-permute-done.4 = f32[256,512]{1,0:T(8,128)S(1)} collective-permute-done((f32[256,512]{1,0:T(8,128)S(1)}, f32[256,512]{1,0:T(8,128)S(1)}, u32[]{:S(2)}, u32[]{:S(2)}) %collective-permute-start.4) | collective-permute-done | bytes 524320 | tf_op jit(solution)/shard_map/ppermute | solution.py:14
  103.2 13.5 %collective-permute-done.5 = f32[256,512]{1,0:T(8,128)S(1)} collective-permute-done((f32[256,512]{1,0:T(8,128)S(1)}, f32[256,512]{1,0:T(8,128)S(1)}, u32[]{:S(2)}, u32[]{:S(2)}) %collective-permute-start.5) | collective-permute-done | bytes 524320 | tf_op jit(solution)/shard_map/ppermute | solution.py:14
  118.8 11.1 %collective-permute-done.6 = f32[256,512]{1,0:T(8,128)S(1)} collective-permute-done((f32[256,512]{1,0:T(8,128)S(1)}, f32[256,512]{1,0:T(8,128)S(1)}, u32[]{:S(2)}, u32[]{:S(2)}) %collective-permute-start.6) | collective-permute-done | bytes 524320 | tf_op jit(solution)/shard_map/ppermute | solution.py:14
  130.6 5.2 collective-permute-start.7
  138.6 2.5 collective-permute-done.8
  143.1 3.7 collective-permute-done.9
  146.8 4.9 collective-permute-start.10
  151.7 4.8 collective-permute-done.10
  156.5 2.6 collective-permute-start.11
  159.1 3.1 collective-permute-done.11
  162.2 2.5 collective-permute-start.12
  165.0 6.0 collective-permute-done.12
  172.7 7.4 %collective-permute-start.13 = (f32[256,512]{1,0:T(8,128)S(1)}, f32[256,512]{1,0:T(8,128)S(1)}, u32[]{:S(2)}, u32[]{:S(2)}) collective-permute-start(f32[256,512]{1,0:T(8,128)S(1)} %convolution_bitcast_fusion.3), channel_id=1, source_target_pairs={{0,1},{1,0},{2,3},{3,2},{4,5},{5,4},{6,7},{7,6},{8,9},{9,8},{10,11... | collective-permute-start | bytes 1572872 | tf_op jit(solution)/shard_map/ppermute | solution.py:14
  183.6 13.1 %collective-permute-done.14 = f32[256,512]{1,0:T(8,128)S(1)} collective-permute-done((f32[256,512]{1,0:T(8,128)S(1)}, f32[256,512]{1,0:T(8,128)S(1)}, u32[]{:S(2)}, u32[]{:S(2)}) %collective-permute-start.14) | collective-permute-done | bytes 524320 | tf_op jit(solution)/shard_map/ppermute | solution.py:14
  198.7 25.9 %collective-permute-done.15 = f32[256,512]{1,0:T(8,128)S(1)} collective-permute-done((f32[256,512]{1,0:T(8,128)S(1)}, f32[256,512]{1,0:T(8,128)S(1)}, u32[]{:S(2)}, u32[]{:S(2)}) %collective-permute-start.15) | collective-permute-done | bytes 524320 | tf_op jit(solution)/shard_map/ppermute | solution.py:14
  224.7 5.3 collective-permute-start.16
  230.0 25.2 %collective-permute-done.16 = f32[256,512]{1,0:T(8,128)S(1)} collective-permute-done((f32[256,512]{1,0:T(8,128)S(1)}, f32[256,512]{1,0:T(8,128)S(1)}, u32[]{:S(2)}, u32[]{:S(2)}) %collective-permute-start.16) | collective-permute-done | bytes 524320 | tf_op jit(solution)/shard_map/ppermute | solution.py:14
  255.3 2.5 collective-permute-start.17
  257.8 12.0 %collective-permute-done.17 = f32[256,512]{1,0:T(8,128)S(1)} collective-permute-done((f32[256,512]{1,0:T(8,128)S(1)}, f32[256,512]{1,0:T(8,128)S(1)}, u32[]{:S(2)}, u32[]{:S(2)}) %collective-permute-start.17) | collective-permute-done | bytes 524320 | tf_op jit(solution)/shard_map/ppermute | solution.py:14
  269.9 3.4 collective-permute-start.18
  273.3 11.7 %collective-permute-done.18 = f32[256,512]{1,0:T(8,128)S(1)} collective-permute-done((f32[256,512]{1,0:T(8,128)S(1)}, f32[256,512]{1,0:T(8,128)S(1)}, u32[]{:S(2)}, u32[]{:S(2)}) %collective-permute-start.18) | collective-permute-done | bytes 524320 | tf_op jit(solution)/shard_map/ppermute | solution.py:14
  285.1 2.4 collective-permute-start.19
  287.5 10.2 %collective-permute-done.19 = f32[256,512]{1,0:T(8,128)S(1)} collective-permute-done((f32[256,512]{1,0:T(8,128)S(1)}, f32[256,512]{1,0:T(8,128)S(1)}, u32[]{:S(2)}, u32[]{:S(2)}) %collective-permute-start.19) | collective-permute-done | bytes 524320 | tf_op jit(solution)/shard_map/ppermute | solution.py:14
  299.8 25.5 %collective-permute-done.20 = f32[256,512]{1,0:T(8,128)S(1)} collective-permute-done((f32[256,512]{1,0:T(8,128)S(1)}, f32[256,512]{1,0:T(8,128)S(1)}, u32[]{:S(2)}, u32[]{:S(2)}) %collective-permute-start.20) | collective-permute-done | bytes 524320 | tf_op jit(solution)/shard_map/ppermute | solution.py:14
  325.9 2.9 collective-permute-start.21
  331.6 2.5 collective-permute-done.22
  336.0 3.4 collective-permute-done.23
  339.4 5.4 collective-permute-start.24
  344.8 3.2 collective-permute-done.24
  348.0 2.8 collective-permute-start.25
  350.8 2.2 collective-permute-done.25
  353.0 5.0 collective-permute-start.26
  358.0 2.7 collective-permute-done.26
  362.8 5.2 collective-permute-done.27
  369.7 8.8 %collective-permute-start.28 = (f32[256,512]{1,0:T(8,128)S(1)}, f32[256,512]{1,0:T(8,128)S(1)}, u32[]{:S(2)}, u32[]{:S(2)}) collective-permute-start(f32[256,512]{1,0:T(8,128)S(1)} %convolution_bitcast_fusion.1), channel_id=1, source_target_pairs={{0,1},{1,0},{2,3},{3,2},{4,5},{5,4},{6,7},{7,6},{8,9},{9,8},{10,11... | collective-permute-start | bytes 1572872 | tf_op jit(solution)/shard_map/ppermute | solution.py:14
  382.0 13.1 %collective-permute-done.29 = f32[256,512]{1,0:T(8,128)S(1)} collective-permute-done((f32[256,512]{1,0:T(8,128)S(1)}, f32[256,512]{1,0:T(8,128)S(1)}, u32[]{:S(2)}, u32[]{:S(2)}) %collective-permute-start.29) | collective-permute-done | bytes 524320 | tf_op jit(solution)/shard_map/ppermute | solution.py:14
  395.2 2.3 collective-permute-start.30
  397.5 25.5 %collective-permute-done.30 = f32[256,512]{1,0:T(8,128)S(1)} collective-permute-done((f32[256,512]{1,0:T(8,128)S(1)}, f32[256,512]{1,0:T(8,128)S(1)}, u32[]{:S(2)}, u32[]{:S(2)}) %collective-permute-start.30) | collective-permute-done | bytes 524320 | tf_op jit(solution)/shard_map/ppermute | solution.py:14
  423.1 5.4 collective-permute-start.31
  428.5 25.1 %collective-permute-done.31 = f32[256,512]{1,0:T(8,128)S(1)} collective-permute-done((f32[256,512]{1,0:T(8,128)S(1)}, f32[256,512]{1,0:T(8,128)S(1)}, u32[]{:S(2)}, u32[]{:S(2)}) %collective-permute-start.31) | collective-permute-done | bytes 524320 | tf_op jit(solution)/shard_map/ppermute | solution.py:14
  453.7 2.7 collective-permute-start.32
  456.4 11.7 %collective-permute-done.32 = f32[256,512]{1,0:T(8,128)S(1)} collective-permute-done((f32[256,512]{1,0:T(8,128)S(1)}, f32[256,512]{1,0:T(8,128)S(1)}, u32[]{:S(2)}, u32[]{:S(2)}) %collective-permute-start.32) | collective-permute-done | bytes 524320 | tf_op jit(solution)/shard_map/ppermute | solution.py:14
  468.2 4.2 collective-permute-start.33
  472.5 10.8 %collective-permute-done.33 = f32[256,512]{1,0:T(8,128)S(1)} collective-permute-done((f32[256,512]{1,0:T(8,128)S(1)}, f32[256,512]{1,0:T(8,128)S(1)}, u32[]{:S(2)}, u32[]{:S(2)}) %collective-permute-start.33) | collective-permute-done | bytes 524320 | tf_op jit(solution)/shard_map/ppermute | solution.py:14
  485.3 10.7 %collective-permute-done.34 = f32[256,512]{1,0:T(8,128)S(1)} collective-permute-done((f32[256,512]{1,0:T(8,128)S(1)}, f32[256,512]{1,0:T(8,128)S(1)}, u32[]{:S(2)}, u32[]{:S(2)}) %collective-permute-start.34) | collective-permute-done | bytes 524320 | tf_op jit(solution)/shard_map/ppermute | solution.py:14
  496.0 3.1 collective-permute-start.35
  499.2 24.7 %collective-permute-done.35 = f32[256,512]{1,0:T(8,128)S(1)} collective-permute-done((f32[256,512]{1,0:T(8,128)S(1)}, f32[256,512]{1,0:T(8,128)S(1)}, u32[]{:S(2)}, u32[]{:S(2)}) %collective-permute-start.35) | collective-permute-done | bytes 524320 | tf_op jit(solution)/shard_map/ppermute | solution.py:14
  526.1 25.1 %collective-permute-done.36 = f32[256,512]{1,0:T(8,128)S(1)} collective-permute-done((f32[256,512]{1,0:T(8,128)S(1)}, f32[256,512]{1,0:T(8,128)S(1)}, u32[]{:S(2)}, u32[]{:S(2)}) %collective-permute-start.36) | collective-permute-done | bytes 524320 | tf_op jit(solution)/shard_map/ppermute | solution.py:14
  551.9 3.4 collective-permute-start.37
  558.0 2.4 collective-permute-done.38
  560.5 2.7 collective-permute-start.39
  563.2 2.5 collective-permute-done.39
  565.8 5.9 collective-permute-start.40
  571.7 2.5 collective-permute-done.40
  574.2 2.6 collective-permute-start.41
  578.8 5.1 collective-permute-start.42
  587.7 3.8 collective-permute-done.43
  591.5 2.5 collective-permute-start.44
  594.1 8.0 %collective-permute-done.44 = f32[128,512]{1,0:T(8,128)S(1)} collective-permute-done((f32[128,512]{1,0:T(8,128)S(1)}, f32[128,512]{1,0:T(8,128)S(1)}, u32[]{:S(2)}, u32[]{:S(2)}) %collective-permute-start.44) | collective-permute-done | bytes 262176 | tf_op jit(solution)/shard_map/ppermute | solution.py:14
  (96 shorter events, 57.8 us)
Async XLA Ops:
  0.0 1.0 copy-start
  2.6 10.3 %collective-permute-start = (f32[256,512]{1,0:T(8,128)S(1)}, f32[256,512]{1,0:T(8,128)S(1)}, u32[]{:S(2)}, u32[]{:S(2)}) collective-permute-start(f32[256,512]{1,0:T(8,128)S(1)} %fusion.47), channel_id=1, source_target_pairs={{0,1},{1,0},{2,3},{3,2},{4,5},{5,4},{6,7},{7,6},{8,9},{9,8},{10,11... | collective-permute-start | bytes 1572872 | tf_op jit(solution)/shard_map/ppermute | solution.py:14
  13.0 15.0 %collective-permute-start.1 = (f32[256,512]{1,0:T(8,128)S(1)}, f32[256,512]{1,0:T(8,128)S(1)}, u32[]{:S(2)}, u32[]{:S(2)}) collective-permute-start(f32[256,512]{1,0:T(8,128)S(1)} %add.63), channel_id=1, source_target_pairs={{0,2},{2,0},{1,3},{3,1},{4,6},{6,4},{5,7},{7,5},{8,10},{10,8},{9,1... | collective-permute-start | bytes 1572872 | tf_op jit(solution)/shard_map/ppermute | solution.py:14
  28.1 27.8 %collective-permute-start.2 = (f32[256,512]{1,0:T(8,128)S(1)}, f32[256,512]{1,0:T(8,128)S(1)}, u32[]{:S(2)}, u32[]{:S(2)}) collective-permute-start(f32[256,512]{1,0:T(8,128)S(1)} %add.64), channel_id=1, source_target_pairs={{0,4},{4,0},{1,5},{5,1},{2,6},{6,2},{3,7},{7,3},{8,12},{12,8},{9,1... | collective-permute-start | bytes 1572872 | tf_op jit(solution)/shard_map/ppermute | solution.py:14
  56.0 30.2 %collective-permute-start.3 = (f32[256,512]{1,0:T(8,128)S(1)}, f32[256,512]{1,0:T(8,128)S(1)}, u32[]{:S(2)}, u32[]{:S(2)}) collective-permute-start(f32[256,512]{1,0:T(8,128)S(1)} %add.65), channel_id=1, source_target_pairs={{0,8},{8,0},{1,9},{9,1},{2,10},{10,2},{3,11},{11,3},{4,12},{12,4},... | collective-permute-start | bytes 1572872 | tf_op jit(solution)/shard_map/ppermute | solution.py:14
  86.3 14.9 %collective-permute-start.4 = (f32[256,512]{1,0:T(8,128)S(1)}, f32[256,512]{1,0:T(8,128)S(1)}, u32[]{:S(2)}, u32[]{:S(2)}) collective-permute-start(f32[256,512]{1,0:T(8,128)S(1)} %add.66), channel_id=1, source_target_pairs={{0,16},{16,0},{1,17},{17,1},{2,18},{18,2},{3,19},{19,3},{4,20},{20... | collective-permute-start | bytes 1572872 | tf_op jit(solution)/shard_map/ppermute | solution.py:14
  101.3 15.5 %collective-permute-start.5 = (f32[256,512]{1,0:T(8,128)S(1)}, f32[256,512]{1,0:T(8,128)S(1)}, u32[]{:S(2)}, u32[]{:S(2)}) collective-permute-start(f32[256,512]{1,0:T(8,128)S(1)} %add.67), channel_id=1, source_target_pairs={{0,32},{32,0},{1,33},{33,1},{2,34},{34,2},{3,35},{35,3},{4,36},{36... | collective-permute-start | bytes 1572872 | tf_op jit(solution)/shard_map/ppermute | solution.py:14
  116.9 13.1 %copy-start.7 = (f32[4,512]{1,0:T(4,128)S(1)}, f32[4,512]{1,0:T(4,128)}, u32[]{:S(2)}) copy-start(f32[4,512]{1,0:T(4,128)} %param.19) | copy-start | bytes 24580
  116.9 13.1 %collective-permute-start.6 = (f32[256,512]{1,0:T(8,128)S(1)}, f32[256,512]{1,0:T(8,128)S(1)}, u32[]{:S(2)}, u32[]{:S(2)}) collective-permute-start(f32[256,512]{1,0:T(8,128)S(1)} %add.68), channel_id=1, source_target_pairs={{0,64},{64,0},{1,65},{65,1},{2,66},{66,2},{3,67},{67,3},{4,68},{68... | collective-permute-start | bytes 1572872 | tf_op jit(solution)/shard_map/ppermute | solution.py:14
  130.6 34.1 %copy-start.1 = (f32[256,512]{1,0:T(8,128)S(1)}, f32[256,512]{1,0:T(8,128)}, u32[]{:S(2)}) copy-start(f32[256,512]{1,0:T(8,128)} %param.10) | copy-start | bytes 1572868
  130.6 6.0 collective-permute-start.7
  136.7 4.5 collective-permute-start.8
  141.2 5.6 collective-permute-start.9
  146.8 9.7 %collective-permute-start.10 = (f32[32,512]{1,0:T(8,128)S(1)}, f32[32,512]{1,0:T(8,128)S(1)}, u32[]{:S(2)}, u32[]{:S(2)}) collective-permute-start(f32[32,512]{1,0:T(8,128)S(1)} %maximum_select_fusion.18), channel_id=1, source_target_pairs={{0,8},{8,0},{1,9},{9,1},{2,10},{10,2},{3,11},{11,3},{4,12},{12,4},... | collective-permute-start | bytes 196616 | tf_op jit(solution)/shard_map/ppermute | solution.py:14
  156.5 5.7 collective-permute-start.11
  162.2 8.8 %copy-start.4 = (f32[256,256]{1,0:T(8,128)S(1)}, f32[256,256]{1,0:T(8,128)}, u32[]{:S(2)}) copy-start(f32[256,256]{1,0:T(8,128)} %param.18) | copy-start | bytes 786436
  162.2 8.8 %collective-permute-start.12 = (f32[128,512]{1,0:T(8,128)S(1)}, f32[128,512]{1,0:T(8,128)S(1)}, u32[]{:S(2)}, u32[]{:S(2)}) collective-permute-start(f32[128,512]{1,0:T(8,128)S(1)} %maximum_select_fusion.12), channel_id=1, source_target_pairs={{0,32},{32,0},{1,33},{33,1},{2,34},{34,2},{3,35},{35,3},{4,36},{36... | collective-permute-start | bytes 786440 | tf_op jit(solution)/shard_map/ppermute | solution.py:14
  165.0 7.0 %copy-start.2 = (f32[256,256]{1,0:T(8,128)S(1)}, f32[256,256]{1,0:T(8,128)}, u32[]{:S(2)}) copy-start(f32[256,256]{1,0:T(8,128)} %param.14) | copy-start | bytes 786436
  172.7 8.9 %collective-permute-start.13 = (f32[256,512]{1,0:T(8,128)S(1)}, f32[256,512]{1,0:T(8,128)S(1)}, u32[]{:S(2)}, u32[]{:S(2)}) collective-permute-start(f32[256,512]{1,0:T(8,128)S(1)} %convolution_bitcast_fusion.3), channel_id=1, source_target_pairs={{0,1},{1,0},{2,3},{3,2},{4,5},{5,4},{6,7},{7,6},{8,9},{9,8},{10,11... | collective-permute-start | bytes 1572872 | tf_op jit(solution)/shard_map/ppermute | solution.py:14
  181.6 15.0 %collective-permute-start.14 = (f32[256,512]{1,0:T(8,128)S(1)}, f32[256,512]{1,0:T(8,128)S(1)}, u32[]{:S(2)}, u32[]{:S(2)}) collective-permute-start(f32[256,512]{1,0:T(8,128)S(1)} %add.69), channel_id=1, source_target_pairs={{0,2},{2,0},{1,3},{3,1},{4,6},{6,4},{5,7},{7,5},{8,10},{10,8},{9,1... | collective-permute-start | bytes 1572872 | tf_op jit(solution)/shard_map/ppermute | solution.py:14
  196.8 27.8 %collective-permute-start.15 = (f32[256,512]{1,0:T(8,128)S(1)}, f32[256,512]{1,0:T(8,128)S(1)}, u32[]{:S(2)}, u32[]{:S(2)}) collective-permute-start(f32[256,512]{1,0:T(8,128)S(1)} %add.70), channel_id=1, source_target_pairs={{0,4},{4,0},{1,5},{5,1},{2,6},{6,2},{3,7},{7,3},{8,12},{12,8},{9,1... | collective-permute-start | bytes 1572872 | tf_op jit(solution)/shard_map/ppermute | solution.py:14
  224.7 30.6 %collective-permute-start.16 = (f32[256,512]{1,0:T(8,128)S(1)}, f32[256,512]{1,0:T(8,128)S(1)}, u32[]{:S(2)}, u32[]{:S(2)}) collective-permute-start(f32[256,512]{1,0:T(8,128)S(1)} %add.71), channel_id=1, source_target_pairs={{0,8},{8,0},{1,9},{9,1},{2,10},{10,2},{3,11},{11,3},{4,12},{12,4},... | collective-permute-start | bytes 1572872 | tf_op jit(solution)/shard_map/ppermute | solution.py:14
  255.3 14.5 %collective-permute-start.17 = (f32[256,512]{1,0:T(8,128)S(1)}, f32[256,512]{1,0:T(8,128)S(1)}, u32[]{:S(2)}, u32[]{:S(2)}) collective-permute-start(f32[256,512]{1,0:T(8,128)S(1)} %add.72), channel_id=1, source_target_pairs={{0,16},{16,0},{1,17},{17,1},{2,18},{18,2},{3,19},{19,3},{4,20},{20... | collective-permute-start | bytes 1572872 | tf_op jit(solution)/shard_map/ppermute | solution.py:14
  269.9 15.1 %collective-permute-start.18 = (f32[256,512]{1,0:T(8,128)S(1)}, f32[256,512]{1,0:T(8,128)S(1)}, u32[]{:S(2)}, u32[]{:S(2)}) collective-permute-start(f32[256,512]{1,0:T(8,128)S(1)} %add.73), channel_id=1, source_target_pairs={{0,32},{32,0},{1,33},{33,1},{2,34},{34,2},{3,35},{35,3},{4,36},{36... | collective-permute-start | bytes 1572872 | tf_op jit(solution)/shard_map/ppermute | solution.py:14
  285.1 12.7 %collective-permute-start.19 = (f32[256,512]{1,0:T(8,128)S(1)}, f32[256,512]{1,0:T(8,128)S(1)}, u32[]{:S(2)}, u32[]{:S(2)}) collective-permute-start(f32[256,512]{1,0:T(8,128)S(1)} %add.74), channel_id=1, source_target_pairs={{0,64},{64,0},{1,65},{65,1},{2,66},{66,2},{3,67},{67,3},{4,68},{68... | collective-permute-start | bytes 1572872 | tf_op jit(solution)/shard_map/ppermute | solution.py:14
  297.8 27.4 %copy-start.8 = (f32[2,512]{1,0:T(2,128)S(1)}, f32[2,512]{1,0:T(2,128)}, u32[]{:S(2)}) copy-start(f32[2,512]{1,0:T(2,128)} %param.16) | copy-start | bytes 12292
  297.8 27.4 %collective-permute-start.20 = (f32[256,512]{1,0:T(8,128)S(1)}, f32[256,512]{1,0:T(8,128)S(1)}, u32[]{:S(2)}, u32[]{:S(2)}) collective-permute-start(f32[256,512]{1,0:T(8,128)S(1)} %add.75), channel_id=1, source_target_pairs={{0,128},{128,0},{1,129},{129,1},{2,130},{130,2},{3,131},{131,3},{4... | collective-permute-start | bytes 1572872 | tf_op jit(solution)/shard_map/ppermute | solution.py:14
  325.9 3.7 collective-permute-start.21
  329.6 4.4 collective-permute-start.22
  334.0 5.4 collective-permute-start.23
  339.4 8.6 %collective-permute-start.24 = (f32[16,512]{1,0:T(8,128)S(1)}, f32[16,512]{1,0:T(8,128)S(1)}, u32[]{:S(2)}, u32[]{:S(2)}) collective-permute-start(f32[16,512]{1,0:T(8,128)S(1)} %maximum_select_fusion.22), channel_id=1, source_target_pairs={{0,8},{8,0},{1,9},{9,1},{2,10},{10,2},{3,11},{11,3},{4,12},{12,4},... | collective-permute-start | bytes 98312 | tf_op jit(solution)/shard_map/ppermute | solution.py:14
  348.0 5.0 collective-permute-start.25
  353.0 15.0 %copy-start.5 = (f32[256,256]{1,0:T(8,128)S(1)}, f32[256,256]{1,0:T(8,128)}, u32[]{:S(2)}) copy-start(f32[256,256]{1,0:T(8,128)} %param.15) | copy-start | bytes 786436
  353.0 7.7 %collective-permute-start.26 = (f32[64,512]{1,0:T(8,128)S(1)}, f32[64,512]{1,0:T(8,128)S(1)}, u32[]{:S(2)}, u32[]{:S(2)}) collective-permute-start(f32[64,512]{1,0:T(8,128)S(1)} %maximum_select_fusion.16), channel_id=1, source_target_pairs={{0,32},{32,0},{1,33},{33,1},{2,34},{34,2},{3,35},{35,3},{4,36},{36... | collective-permute-start | bytes 393224 | tf_op jit(solution)/shard_map/ppermute | solution.py:14
  360.7 8.3 %copy-start.3 = (f32[256,256]{1,0:T(8,128)S(1)}, f32[256,256]{1,0:T(8,128)}, u32[]{:S(2)}) copy-start(f32[256,256]{1,0:T(8,128)} %param.11) | copy-start | bytes 786436
  360.7 7.2 %collective-permute-start.27 = (f32[128,512]{1,0:T(8,128)S(1)}, f32[128,512]{1,0:T(8,128)S(1)}, u32[]{:S(2)}, u32[]{:S(2)}) collective-permute-start(f32[128,512]{1,0:T(8,128)S(1)} %maximum_select_fusion.13), channel_id=1, source_target_pairs={{0,64},{64,0},{1,65},{65,1},{2,66},{66,2},{3,67},{67,3},{4,68},{68... | collective-permute-start | bytes 786440 | tf_op jit(solution)/shard_map/ppermute | solution.py:14
  369.7 10.4 %collective-permute-start.28 = (f32[256,512]{1,0:T(8,128)S(1)}, f32[256,512]{1,0:T(8,128)S(1)}, u32[]{:S(2)}, u32[]{:S(2)}) collective-permute-start(f32[256,512]{1,0:T(8,128)S(1)} %convolution_bitcast_fusion.1), channel_id=1, source_target_pairs={{0,1},{1,0},{2,3},{3,2},{4,5},{5,4},{6,7},{7,6},{8,9},{9,8},{10,11... | collective-permute-start | bytes 1572872 | tf_op jit(solution)/shard_map/ppermute | solution.py:14
  380.1 15.0 %collective-permute-start.29 = (f32[256,512]{1,0:T(8,128)S(1)}, f32[256,512]{1,0:T(8,128)S(1)}, u32[]{:S(2)}, u32[]{:S(2)}) collective-permute-start(f32[256,512]{1,0:T(8,128)S(1)} %add.76), channel_id=1, source_target_pairs={{0,2},{2,0},{1,3},{3,1},{4,6},{6,4},{5,7},{7,5},{8,10},{10,8},{9,1... | collective-permute-start | bytes 1572872 | tf_op jit(solution)/shard_map/ppermute | solution.py:14
  395.2 27.8 %collective-permute-start.30 = (f32[256,512]{1,0:T(8,128)S(1)}, f32[256,512]{1,0:T(8,128)S(1)}, u32[]{:S(2)}, u32[]{:S(2)}) collective-permute-start(f32[256,512]{1,0:T(8,128)S(1)} %add.77), channel_id=1, source_target_pairs={{0,4},{4,0},{1,5},{5,1},{2,6},{6,2},{3,7},{7,3},{8,12},{12,8},{9,1... | collective-permute-start | bytes 1572872 | tf_op jit(solution)/shard_map/ppermute | solution.py:14
  423.1 30.5 %collective-permute-start.31 = (f32[256,512]{1,0:T(8,128)S(1)}, f32[256,512]{1,0:T(8,128)S(1)}, u32[]{:S(2)}, u32[]{:S(2)}) collective-permute-start(f32[256,512]{1,0:T(8,128)S(1)} %add.78), channel_id=1, source_target_pairs={{0,8},{8,0},{1,9},{9,1},{2,10},{10,2},{3,11},{11,3},{4,12},{12,4},... | collective-permute-start | bytes 1572872 | tf_op jit(solution)/shard_map/ppermute | solution.py:14
  453.7 14.4 %collective-permute-start.32 = (f32[256,512]{1,0:T(8,128)S(1)}, f32[256,512]{1,0:T(8,128)S(1)}, u32[]{:S(2)}, u32[]{:S(2)}) collective-permute-start(f32[256,512]{1,0:T(8,128)S(1)} %add.79), channel_id=1, source_target_pairs={{0,16},{16,0},{1,17},{17,1},{2,18},{18,2},{3,19},{19,3},{4,20},{20... | collective-permute-start | bytes 1572872 | tf_op jit(solution)/shard_map/ppermute | solution.py:14
  468.2 15.0 %collective-permute-start.33 = (f32[256,512]{1,0:T(8,128)S(1)}, f32[256,512]{1,0:T(8,128)S(1)}, u32[]{:S(2)}, u32[]{:S(2)}) collective-permute-start(f32[256,512]{1,0:T(8,128)S(1)} %add.80), channel_id=1, source_target_pairs={{0,32},{32,0},{1,33},{33,1},{2,34},{34,2},{3,35},{35,3},{4,36},{36... | collective-permute-start | bytes 1572872 | tf_op jit(solution)/shard_map/ppermute | solution.py:14
  483.3 12.6 %collective-permute-start.34 = (f32[256,512]{1,0:T(8,128)S(1)}, f32[256,512]{1,0:T(8,128)S(1)}, u32[]{:S(2)}, u32[]{:S(2)}) collective-permute-start(f32[256,512]{1,0:T(8,128)S(1)} %add.81), channel_id=1, source_target_pairs={{0,64},{64,0},{1,65},{65,1},{2,66},{66,2},{3,67},{67,3},{4,68},{68... | collective-permute-start | bytes 1572872 | tf_op jit(solution)/shard_map/ppermute | solution.py:14
  496.0 27.9 %collective-permute-start.35 = (f32[256,512]{1,0:T(8,128)S(1)}, f32[256,512]{1,0:T(8,128)S(1)}, u32[]{:S(2)}, u32[]{:S(2)}) collective-permute-start(f32[256,512]{1,0:T(8,128)S(1)} %add.82), channel_id=1, source_target_pairs={{0,128},{128,0},{1,129},{129,1},{2,130},{130,2},{3,131},{131,3},{4... | collective-permute-start | bytes 1572872 | tf_op jit(solution)/shard_map/ppermute | solution.py:14
  524.0 27.3 %collective-permute-start.36 = (f32[256,512]{1,0:T(8,128)S(1)}, f32[256,512]{1,0:T(8,128)S(1)}, u32[]{:S(2)}, u32[]{:S(2)}) collective-permute-start(f32[256,512]{1,0:T(8,128)S(1)} %add.83), channel_id=1, source_target_pairs={{0,256},{256,0},{1,257},{257,1},{2,258},{258,2},{3,259},{259,3},{4... | collective-permute-start | bytes 1572872 | tf_op jit(solution)/shard_map/ppermute | solution.py:14
  526.1 25.2 %copy-start.9 = (f32[1,512]{1,0:T(1,128)S(1)}, f32[1,512]{1,0:T(1,128)}, u32[]{:S(2)}) copy-start(f32[1,512]{1,0:T(1,128)} %param.13) | copy-start | bytes 6148
  551.9 4.2 collective-permute-start.37
  556.1 4.4 collective-permute-start.38
  560.5 5.3 collective-permute-start.39
  565.8 8.4 %collective-permute-start.40 = (f32[8,512]{1,0:T(8,128)S(1)}, f32[8,512]{1,0:T(8,128)S(1)}, u32[]{:S(2)}, u32[]{:S(2)}) collective-permute-start(f32[8,512]{1,0:T(8,128)S(1)} %maximum_select_fusion.26), channel_id=1, source_target_pairs={{0,8},{8,0},{1,9},{9,1},{2,10},{10,2},{3,11},{11,3},{4,12},{12,4},... | collective-permute-start | bytes 49160 | tf_op jit(solution)/shard_map/ppermute | solution.py:14
  574.2 4.6 collective-permute-start.41
  578.8 6.8 %collective-permute-start.42 = (f32[32,512]{1,0:T(8,128)S(1)}, f32[32,512]{1,0:T(8,128)S(1)}, u32[]{:S(2)}, u32[]{:S(2)}) collective-permute-start(f32[32,512]{1,0:T(8,128)S(1)} %maximum_select_fusion.20), channel_id=1, source_target_pairs={{0,32},{32,0},{1,33},{33,1},{2,34},{34,2},{3,35},{35,3},{4,36},{36... | collective-permute-start | bytes 196616 | tf_op jit(solution)/shard_map/ppermute | solution.py:14
  585.6 16.4 %copy-start.6 = (f32[256,256]{1,0:T(8,128)S(1)}, f32[256,256]{1,0:T(8,128)}, u32[]{:S(2)}) copy-start(f32[256,256]{1,0:T(8,128)} %param.12) | copy-start | bytes 786436
  585.7 5.8 collective-permute-start.43
  591.5 10.6 %collective-permute-start.44 = (f32[128,512]{1,0:T(8,128)S(1)}, f32[128,512]{1,0:T(8,128)S(1)}, u32[]{:S(2)}, u32[]{:S(2)}) collective-permute-start(f32[128,512]{1,0:T(8,128)S(1)} %maximum_select_fusion.14), channel_id=1, source_target_pairs={{0,128},{128,0},{1,129},{129,1},{2,130},{130,2},{3,131},{131,3},{4... | collective-permute-start | bytes 786440 | tf_op jit(solution)/shard_map/ppermute | solution.py:14
where the time goes:
time: 613 us; the launch traced here: 604 us
  waiting for transfers between devices  442 us (72%)
  starting transfers between devices  149 us (24%)
  matrix products  8.04 us (1%)
    ppermute x45, waiting for transfers between devices, from_partner(): return lax.ppermute(block, axis, route)  442 us
    ppermute x45, starting transfers between devices, from_partner(): return lax.ppermute(block, axis, route)  149 us
  transfers between devices with their start and end apart: 45, of which 45 were waited for; matrix products, arithmetic and copies ran while one was open for 0% of the time, Pallas kernels for 0%

commit v1 on v0

v1 whole, which is shorter than its diff:
```python
import jax
import jax.numpy as jnp
from jax import lax
from jax.experimental import pallas as pl
from jax.experimental.pallas import tpu as pltpu
from jax.sharding import PartitionSpec as P

MESH = pl.DeviceIdType.MESH
F32 = jnp.float32
NX, NZ, NC, NY = 4, 8, 2, 8
K, N, R = 256, 512, 8


def dot(a, b, dims=((1,), (0,))):
    return lax.dot_general(
        a, b, (dims, ((), ())), precision=lax.Precision.HIGHEST, preferred_element_type=F32
    )


def pick(rows_of, source_rows):
    row = lax.broadcasted_iota(jnp.int32, (K, source_rows), 0)
    column = lax.broadcasted_iota(jnp.int32, (K, source_rows), 1)
    return (column == rows_of(row)).astype(F32)


def slot_row(member):
    return 8 * ((member % 2) * 32 + member // 2)


def kernel(
    x_ref, v0_ref, w0_ref, cap0_ref, v1_ref, w1_ref, cap1_ref, v2_ref, w2_ref, cap2_ref,
    out_ref,
    gram, q2, q10, gram_c, q2_c, q10_c, gram_x, q2_x, q10_x, gram_z, q2_z, q10_z,
    gram_all, cap_all, c2_all, c1_all, c0_all,
    cap1_y, cap0_y, q2_y, q1_y, q0_y,
    send_sem, recv_sem,
):
    me = lax.axis_index("rows")
    y, x, z, c = me // 64, (me // 16) % 4, (me // 2) % 8, me % 2
    other = 1 - c
    half = pl.multiple_of(c * 256, 256)
    other_half = pl.multiple_of(other * 256, 256)
    block = pl.multiple_of(c * 256 + x * 64, 64)
    own = pl.multiple_of(c * 256 + x * 64 + z * 8, 8)

    def at(yy, xx, zz, cc):
        return ((yy * 4 + xx) * 8 + zz) * 2 + cc

    def flip(k):
        b0, b1, b2 = y % 2, (y // 2) % 2, y // 4
        b0 = 1 - b0 if k & 1 else b0
        b1 = 1 - b1 if k & 2 else b1
        b2 = 1 - b2 if k & 4 else b2
        return b2 * 4 + b1 * 2 + b0

    core = at(y, x, z, other)
    along_x = [((x + k) % 4, at(y, (x + k) % 4, z, c)) for k in range(1, 4)]
    along_z = [((z + k) % 8, at(y, x, (z + k) % 8, c)) for k in range(1, 8)]
    along_y = [at(flip(k), x, z, c) for k in range(1, 8)]

    barrier = pltpu.get_barrier_semaphore()
    everyone = [core] + [d for _, d in along_x] + [d for _, d in along_z] + along_y
    for device in everyone:
        pl.semaphore_signal(barrier, inc=1, device_id=(device,), device_id_type=MESH)

    used = [0]
    started = []

    def send(source, target, device):
        index = used[0]
        used[0] += 1
        copy = pltpu.make_async_remote_copy(
            src_ref=source,
            dst_ref=target,
            send_sem=send_sem.at[index],
            recv_sem=recv_sem.at[index],
            device_id=(device,),
            device_id_type=MESH,
        )
        copy.start()
        started.append(copy)
        return copy

    def arrived(copies):
        for copy in copies:
            copy.wait_recv()

    def core_step(buffer, landing):
        return [send(buffer.at[pl.ds(other_half, 256)], landing, core)]

    def core_sum(buffer, landing, copies):
        arrived(copies)
        buffer[pl.ds(half, 256), :] += landing[...]

    def x_step(buffer, landing):
        return [
            send(
                buffer.at[pl.ds(pl.multiple_of(c * 256 + xx * 64, 64), 64)], landing.at[k], device
            )
            for k, (xx, device) in enumerate(along_x)
        ]

    def x_sum(buffer, landing, copies):
        arrived(copies)
        buffer[pl.ds(block, 64), :] += landing[0] + landing[1] + landing[2]

    def z_step(buffer, landing):
        return [
            send(
                buffer.at[pl.ds(pl.multiple_of(c * 256 + x * 64 + zz * 8, 8), 8)],
                landing.at[k],
                device,
            )
            for k, (zz, device) in enumerate(along_z)
        ]

    def z_sum(buffer, landing, copies):
        arrived(copies)
        total = buffer[pl.ds(own, 8), :]
        for k in range(7):
            total = total + landing[k]
        return total

    def gather_z(full):
        part = full.at[pl.ds(own, 8)]
        return [send(part, part, device) for _, device in along_z]

    def gather_x(full, copies):
        arrived(copies)
        part = full.at[pl.ds(block, 64)]
        return [send(part, part, device) for _, device in along_x]

    def gather_core(full, copies):
        arrived(copies)
        part = full.at[pl.ds(half, 256)]
        return [send(part, part, core)]

    w2_t, w1_t = w2_ref[...].T, w1_ref[...].T
    gram[0:256, 0:256] = dot(w2_t, v1_ref[...])
    gram[256:512, 0:256] = dot(w2_t, v0_ref[...])
    cross = dot(w1_t, v0_ref[...])
    gram[0:256, 256:384] = cross[:, 0:128]
    gram[256:512, 256:384] = cross[:, 128:256]

    cap1_y[y % 2] = cap1_ref[...]
    cap0_y[y % 4] = cap0_ref[...]

    pl.semaphore_wait(barrier, len(everyone))
    gram_copies = core_step(gram, gram_c)

    x_t = x_ref[...].T
    q2[...] = dot(x_t, v2_ref[...])
    q2_copies = core_step(q2, q2_c)
    cap_copies = [send(cap1_ref, cap1_y.at[y % 2], along_y[0])]
    cap_copies += [send(cap0_ref, cap0_y.at[y % 4], along_y[k]) for k in range(3)]
    core_sum(gram, gram_c, gram_copies)
    gram_copies = x_step(gram, gram_x)
    core_sum(q2, q2_c, q2_copies)
    q2_copies = x_step(q2, q2_x)

    q10[:, 0:256] = dot(x_t, v1_ref[...])
    q10[:, 256:512] = dot(x_t, v0_ref[...])
    q10_copies = core_step(q10, q10_c)

    arrived(cap_copies)
    rows = pl.ds(own, 8)
    lower = jnp.concatenate([cap2_ref[...], cap1_y[0], cap1_y[1]], axis=0)
    upper = jnp.concatenate(
        [cap0_y[t][:, 0:256] for t in range(4)] + [cap0_y[t][:, 256:512] for t in range(4)], axis=0
    )
    cap_all[rows, 0:512] = lower
    cap_all[rows, 512:768] = upper
    cap_copies = gather_z(cap_all)

    core_sum(q10, q10_c, q10_copies)
    x_sum(gram, gram_x, gram_copies)
    gram_copies = z_step(gram, gram_z)
    x_sum(q2, q2_x, q2_copies)
    q2_copies = z_step(q2, q2_z)
    q10_copies = x_step(q10, q10_x)
    cap_copies = gather_x(cap_all, cap_copies)

    gram_all[rows, :] = z_sum(gram, gram_z, gram_copies)
    gram_copies = gather_z(gram_all)
    q2_y[y % 2] = z_sum(q2, q2_z, q2_copies)
    q2_copies = [send(q2_y.at[y % 2], q2_y.at[y % 2], along_y[0])]
    x_sum(q10, q10_x, q10_copies)
    q10_copies = z_step(q10, q10_z)
    cap_copies = gather_core(cap_all, cap_copies)
    gram_copies = gather_x(gram_all, gram_copies)

    q10_own = z_sum(q10, q10_z, q10_copies)
    q1_own, q0_own = q10_own[:, 0:256], q10_own[:, 256:512]

    arrived(cap_copies)
    caps = cap_all[:, 0:512]
    cap2 = dot(pick(lambda i: slot_row(i // 4) + i % 4, N), caps)
    arrived(q2_copies)
    c2 = dot(jnp.concatenate([q2_y[1], q2_y[0]], axis=1), cap2, ((1,), (1,)))
    c2_all[rows, :] = c2
    c2_copies = gather_z(c2_all)
    gram_copies = gather_core(gram_all, gram_copies)
    cap1 = dot(pick(lambda i: slot_row((i % 128) // 2) + 4 + 2 * (i // 128) + i % 2, N), caps)

    arrived(gram_copies)
    q1_y[y % 4] = q1_own - dot(c2, gram_all[0:256, 0:256])
    q1_copies = [send(q1_y.at[y % 4], q1_y.at[y % 4], along_y[k]) for k in range(3)]
    q0_own = q0_own - dot(c2, gram_all[256:512, 0:256])
    caps = cap_all[:, 512:768]
    cap0 = jnp.concatenate(
        [dot(pick(lambda i: slot_row(i % 64) + 4 * s + i // 64, N), caps) for s in range(2)], axis=1
    )
    c2_copies = gather_x(c2_all, c2_copies)
    cross = jnp.concatenate([gram_all[0:256, 256:384], gram_all[256:512, 256:384]], axis=1)

    arrived(q1_copies)
    c1 = dot(
        jnp.concatenate([q1_y[2] + q1_y[3], q1_y[0] + q1_y[1]], axis=1), cap1, ((1,), (1,))
    )
    c1_all[rows, :] = c1
    q0_y[y] = q0_own - dot(c1, cross)
    q0_copies = [send(q0_y.at[y], q0_y.at[y], along_y[k]) for k in range(7)]
    c1_copies = gather_z(c1_all)
    c2_copies = gather_core(c2_all, c2_copies)
    c1_copies = gather_x(c1_all, c1_copies)

    arrived(q0_copies)
    c0 = dot(
        jnp.concatenate(
            [(q0_y[4] + q0_y[5]) + (q0_y[6] + q0_y[7]), (q0_y[0] + q0_y[1]) + (q0_y[2] + q0_y[3])],
            axis=1,
        ),
        cap0,
        ((1,), (1,)),
    )
    c0_all[rows, :] = c0
    c0_copies = gather_z(c0_all)
    arrived(c2_copies)
    state = x_ref[...] - dot(w2_ref[...], c2_all[...], ((1,), (1,)))
    c1_copies = gather_core(c1_all, c1_copies)
    c0_copies = gather_x(c0_all, c0_copies)
    arrived(c1_copies)
    state = state - dot(w1_ref[...], c1_all[...], ((1,), (1,)))
    c0_copies = gather_core(c0_all, c0_copies)
    arrived(c0_copies)
    out_ref[...] = state - dot(w0_ref[...], c0_all[...], ((1,), (1,)))
    for copy in started:
        copy.wait_send()


def shards(
    rhs, v_basis0, w_basis0, cap_inv0, v_basis1, w_basis1, cap_inv1, v_basis2, w_basis2, cap_inv2
):
    vmem = pl.BlockSpec(memory_space=pltpu.VMEM)
    copies = 180

    def f32(*shape):
        return pltpu.VMEM(shape, F32)

    return pl.pallas_call(
        kernel,
        out_shape=jax.ShapeDtypeStruct(rhs.shape, F32),
        in_specs=[vmem] * 10,
        out_specs=vmem,
        scratch_shapes=[
            f32(512, 384), f32(512, 256), f32(512, 512),
            f32(256, 384), f32(256, 256), f32(256, 512),
            f32(3, 64, 384), f32(3, 64, 256), f32(3, 64, 512),
            f32(7, 8, 384), f32(7, 8, 256), f32(7, 8, 512),
            f32(512, 384), f32(512, 768), f32(512, 256), f32(512, 256), f32(512, 256),
            f32(2, 2, 512), f32(4, 1, 512), f32(2, 8, 256), f32(4, 8, 256), f32(8, 8, 256),
            pltpu.SemaphoreType.DMA((copies,)),
            pltpu.SemaphoreType.DMA((copies,)),
        ],
        compiler_params=pltpu.CompilerParams(
            collective_id=0, has_side_effects=True, vmem_limit_bytes=48 << 20
        ),
    )(rhs, v_basis0, w_basis0, cap_inv0, v_basis1, w_basis1, cap_inv1, v_basis2, w_basis2, cap_inv2)


def solution(mesh):
    rows = P("rows", None)
    return jax.shard_map(
        shards, mesh=mesh, in_specs=(rows,) * 10, out_specs=rows, check_vma=False
    )
```

time: 613 us -> 86.7 us (0.14); the launches traced: 604 us -> 86.3 us
  waiting for transfers between devices: 442 us -> 0 us
  starting transfers between devices: 149 us -> 0 us
  Pallas kernels: 0 us -> 76.7 us
  matrix products: 8.04 us -> 0 us
  local copies, waits for them, and re-layouts: 2.2 us -> 9.6 us
    ppermute x45 -> x0, waiting for transfers between devices: 442 us -> none  [from_partner(): return lax.ppermute(block, axis, route)]
    ppermute x45 -> x0, starting transfers between devices: 149 us -> none  [from_partner(): return lax.ppermute(block, axis, route)]
    pallas_call x0 -> x1, Pallas kernels: none -> 76.7 us  [shards(): pl.pallas_call(kernel, out_shape=jax.ShapeDtypeStruct(rhs.shape, F32), in...]
    unnamed x21, local copies, waits for them, and re-layouts: 1.2 us -> 9.6 us
    dot_general x9 -> x0, matrix products: 8.04 us -> none  [the longest x3 2.99 us: apply_level(): jnp.dot(w_basis, coef, precision=lax.Precision.HIGHEST, preferred_element...]
  transfers between devices with their start and end apart: 45 -> 0, of which waited for: 45 -> 0; matrix products, arithmetic and copies ran while one was open for 0% -> 0% of each run, Pallas kernels for 0% -> 0%
where the time goes in v1:
time: 86.7 us; the launch traced here: 86.3 us
  Pallas kernels  76.7 us (88%)
  local copies, waits for them, and re-layouts  9.6 us (11%)
    pallas_call x1, Pallas kernels, shards(): pl.pallas_call(kernel, out_shape=jax.ShapeDtypeStruct(rhs.shape, F32), in...  76.7 us
    unnamed x21, local copies, waits for them, and re-layouts  9.6 us

profile of v1, /device:TPU:1, one launch (start us, length us, event | category | flops | bytes accessed | tf_op | source)
XLA Modules:
  0.0 86.3 jit_solution(16845198583559259398)
XLA Ops:
  0.0 0.0 copy-start
  0.0 1.0 %copy-done = f32[256,512]{1,0:T(8,128)S(1)} copy-done((f32[256,512]{1,0:T(8,128)S(1)}, f32[256,512]{1,0:T(8,128)}, u32[]{:S(2)}) %copy-start) | copy-done | bytes 524312
  1.0 0.0 copy-start.1
  1.0 0.9 %copy-done.1 = f32[256,256]{1,0:T(8,128)S(1)} copy-done((f32[256,256]{1,0:T(8,128)S(1)}, f32[256,256]{1,0:T(8,128)}, u32[]{:S(2)}) %copy-start.1) | copy-done | bytes 262168
  2.0 0.0 copy-start.2
  2.0 0.9 %copy-done.2 = f32[256,256]{1,0:T(8,128)S(1)} copy-done((f32[256,256]{1,0:T(8,128)S(1)}, f32[256,256]{1,0:T(8,128)}, u32[]{:S(2)}) %copy-start.2) | copy-done | bytes 262168
  2.9 0.0 copy-start.3
  2.9 0.9 %copy-done.3 = f32[256,256]{1,0:T(8,128)S(1)} copy-done((f32[256,256]{1,0:T(8,128)S(1)}, f32[256,256]{1,0:T(8,128)}, u32[]{:S(2)}) %copy-start.3) | copy-done | bytes 262168
  3.9 0.0 copy-start.4
  3.9 0.9 %copy-done.4 = f32[256,256]{1,0:T(8,128)S(1)} copy-done((f32[256,256]{1,0:T(8,128)S(1)}, f32[256,256]{1,0:T(8,128)}, u32[]{:S(2)}) %copy-start.4) | copy-done | bytes 262168
  4.8 0.0 copy-start.5
  4.8 0.9 %copy-done.5 = f32[256,256]{1,0:T(8,128)S(1)} copy-done((f32[256,256]{1,0:T(8,128)S(1)}, f32[256,256]{1,0:T(8,128)}, u32[]{:S(2)}) %copy-start.5) | copy-done | bytes 262168
  5.8 0.0 copy-start.6
  5.8 0.9 %copy-done.6 = f32[256,256]{1,0:T(8,128)S(1)} copy-done((f32[256,256]{1,0:T(8,128)S(1)}, f32[256,256]{1,0:T(8,128)}, u32[]{:S(2)}) %copy-start.6) | copy-done | bytes 262168
  6.7 0.0 copy-start.7
  6.7 0.7 copy-done.7
  7.4 0.0 copy-start.8
  7.4 0.7 copy-done.8
  8.1 0.0 copy-start.9
  8.1 0.7 copy-done.9
  8.8 76.7 %shard_map.100 = f32[256,512]{1,0:T(8,128)S(1)} custom-call(f32[256,512]{1,0:T(8,128)S(1)} %copy-done, f32[256,256]{1,0:T(8,128)S(1)} %copy-done.1, f32[256,256]{1,0:T(8,128)S(1)} %copy-done.2, f32[1,512]{1,0:T(1,128)S(1)} %copy-done.9, f32[256,256]{1,0:T(8,128)S(1)} %copy-done.3, f32[256,256]{1,0:T(8,128)S(1)} %copy-done.4, f32[2,512]{1,0:T(2,128)S(1)} %copy-done.8, ...), custom_call_target="tpu_custom_call" | custom-call | tf_op jit(solution)/shard_map/pallas_call | solution.py:260
  85.5 0.8 copy.12
Async XLA Ops:
  0.0 1.0 %copy-start = (f32[256,512]{1,0:T(8,128)S(1)}, f32[256,512]{1,0:T(8,128)}, u32[]{:S(2)}) copy-start(f32[256,512]{1,0:T(8,128)} %x_ref.1) | copy-start | bytes 1572868
  1.0 0.9 %copy-start.1 = (f32[256,256]{1,0:T(8,128)S(1)}, f32[256,256]{1,0:T(8,128)}, u32[]{:S(2)}) copy-start(f32[256,256]{1,0:T(8,128)} %v0_ref.1) | copy-start | bytes 786436
  2.0 0.9 %copy-start.2 = (f32[256,256]{1,0:T(8,128)S(1)}, f32[256,256]{1,0:T(8,128)}, u32[]{:S(2)}) copy-start(f32[256,256]{1,0:T(8,128)} %w0_ref.1) | copy-start | bytes 786436
  2.9 0.9 %copy-start.3 = (f32[256,256]{1,0:T(8,128)S(1)}, f32[256,256]{1,0:T(8,128)}, u32[]{:S(2)}) copy-start(f32[256,256]{1,0:T(8,128)} %v1_ref.1) | copy-start | bytes 786436
  3.9 0.9 %copy-start.4 = (f32[256,256]{1,0:T(8,128)S(1)}, f32[256,256]{1,0:T(8,128)}, u32[]{:S(2)}) copy-start(f32[256,256]{1,0:T(8,128)} %w1_ref.1) | copy-start | bytes 786436
  4.8 0.9 %copy-start.5 = (f32[256,256]{1,0:T(8,128)S(1)}, f32[256,256]{1,0:T(8,128)}, u32[]{:S(2)}) copy-start(f32[256,256]{1,0:T(8,128)} %v2_ref.1) | copy-start | bytes 786436
  5.8 0.9 %copy-start.6 = (f32[256,256]{1,0:T(8,128)S(1)}, f32[256,256]{1,0:T(8,128)}, u32[]{:S(2)}) copy-start(f32[256,256]{1,0:T(8,128)} %w2_ref.1) | copy-start | bytes 786436
  6.7 0.7 copy-start.7
  7.4 0.7 copy-start.8
  8.1 0.7 copy-start.9

commit v2 on v1

v2 whole, which is shorter than its diff:
```python
import jax
import jax.numpy as jnp
from jax import lax
from jax.experimental import pallas as pl
from jax.experimental.pallas import tpu as pltpu
from jax.sharding import PartitionSpec as P

MESH = pl.DeviceIdType.MESH
F32, BF16 = jnp.float32, jnp.bfloat16
NX, NZ, NC, NY = 4, 8, 2, 8
K, N, R = 256, 512, 8


def split(a):
    high = a.astype(BF16)
    return high, (a - high.astype(F32)).astype(BF16)


def part(a, b, dims):
    return lax.dot_general(a, b, (dims, ((), ())), preferred_element_type=F32)


def dot(a, b, dims=((1,), (0,))):
    (a_high, a_low), (b_high, b_low) = a, b
    return part(a_high, b_high, dims) + (part(a_high, b_low, dims) + part(a_low, b_high, dims))


def few_rows_dot(a, b, dims=((1,), (0,))):
    (a_high, a_low), (b_high, b_low) = split(a), b
    both = part(jnp.concatenate([a_high, a_low], axis=0), b_high, dims)
    return both[0:R] + (both[R:] + part(a_high, b_low, dims))


def pick(count, rows_of, pieces):
    row = lax.broadcasted_iota(jnp.int32, (count, N), 0)
    column = lax.broadcasted_iota(jnp.int32, (count, N), 1)
    chosen = (column == rows_of(row)).astype(F32).astype(BF16)
    return part(chosen, pieces, ((1,), (0,))).astype(BF16)


def paired_rows(rows_of, first, second):
    pieces = jnp.concatenate(split(jnp.concatenate([first, second], axis=1)), axis=1)
    quarters = [pick(128, lambda i: rows_of(i) + q, pieces) for q in range(4)]

    def matrix(start):
        upper = jnp.concatenate([q[:, start : start + 128] for q in quarters], axis=1)
        lower = jnp.concatenate([q[:, start + 128 : start + 256] for q in quarters], axis=1)
        return jnp.concatenate([upper, lower], axis=0)

    return matrix(0), matrix(256)


def slot_row(member):
    return 8 * ((member % 2) * 32 + member // 2)


def kernel(
    x_hbm, v0_hbm, w0_hbm, cap0_hbm, v1_hbm, w1_hbm, cap1_hbm, v2_hbm, w2_hbm, cap2_hbm,
    out_ref,
    x_ref, v0_ref, w0_ref, cap0_ref, v1_ref, w1_ref, cap1_ref, v2_ref, w2_ref, cap2_ref, load_sem,
    gram, gram_c, gram_z, gram_x, gram_all,
    q2, cross, q10, q2_c, cross_c, q10_c, q2_x, cross_x, q10_x, q2_z, cross_z, q10_z,
    cross_all, cap2_all, cap10_all, cap10_y, c2_all, c1_all, c0_all,
    cap0_y, q2_y, q1_y, q0_y,
    send_sem, recv_sem,
):
    me = lax.axis_index("rows")
    y, x, z, c = me // 64, (me // 16) % 4, (me // 2) % 8, me % 2
    other = 1 - c
    half = pl.multiple_of(c * 256, 256)
    other_half = pl.multiple_of(other * 256, 256)
    block = pl.multiple_of(c * 256 + x * 64, 64)
    own = pl.multiple_of(c * 256 + x * 64 + z * 8, 8)

    def at(yy, xx, zz, cc):
        return ((yy * 4 + xx) * 8 + zz) * 2 + cc

    def flip(k):
        b0, b1, b2 = y % 2, (y // 2) % 2, y // 4
        b0 = 1 - b0 if k & 1 else b0
        b1 = 1 - b1 if k & 2 else b1
        b2 = 1 - b2 if k & 4 else b2
        return b2 * 4 + b1 * 2 + b0

    core = at(y, x, z, other)
    along_x = [((x + k) % 4, at(y, (x + k) % 4, z, c)) for k in range(1, 4)]
    along_z = [((z + k) % 8, at(y, x, (z + k) % 8, c)) for k in range(1, 8)]
    along_y = [at(flip(k), x, z, c) for k in range(1, 8)]

    barrier = pltpu.get_barrier_semaphore()
    everyone = [core] + [d for _, d in along_x] + [d for _, d in along_z] + along_y
    for device in everyone:
        pl.semaphore_signal(barrier, inc=1, device_id=(device,), device_id_type=MESH)

    loads = {}
    for index, (name, source, target) in enumerate(
        [
            ("w2", w2_hbm, w2_ref), ("v1", v1_hbm, v1_ref), ("cap2", cap2_hbm, cap2_ref),
            ("cap0", cap0_hbm, cap0_ref), ("cap1", cap1_hbm, cap1_ref), ("x", x_hbm, x_ref),
            ("v2", v2_hbm, v2_ref), ("v0", v0_hbm, v0_ref), ("w1", w1_hbm, w1_ref),
            ("w0", w0_hbm, w0_ref),
        ]
    ):
        loads[name] = pltpu.make_async_copy(source, target, load_sem.at[index])
        loads[name].start()

    used = [0]
    sent = []

    def group(moves, size_like):
        index = used[0]
        used[0] += 1
        for source, target, device in moves:
            pltpu.make_async_remote_copy(
                src_ref=source,
                dst_ref=target,
                send_sem=send_sem.at[index],
                recv_sem=recv_sem.at[index],
                device_id=(device,),
                device_id_type=MESH,
            ).start()
        sent.append((index, size_like))
        return index, size_like

    def arrived(one_group):
        index, size_like = one_group
        pltpu.make_async_copy(size_like, size_like, recv_sem.at[index]).wait()

    def left():
        for index, size_like in sent:
            pltpu.make_async_copy(size_like, size_like, send_sem.at[index]).wait()
        sent.clear()

    def core_step(buffer, landing):
        return group([(buffer.at[pl.ds(other_half, 256)], landing, core)], landing)

    def core_sum(buffer, landing, copies):
        arrived(copies)
        buffer[pl.ds(half, 256), :] += landing[...]

    def x_step(buffer, landing):
        return group(
            [
                (
                    buffer.at[pl.ds(pl.multiple_of(c * 256 + xx * 64, 64), 64)],
                    landing.at[k],
                    device,
                )
                for k, (xx, device) in enumerate(along_x)
            ],
            landing,
        )

    def x_sum(buffer, landing, copies):
        arrived(copies)
        buffer[pl.ds(block, 64), :] += landing[0] + landing[1] + landing[2]

    def z_step(buffer, landing):
        return group(
            [
                (
                    buffer.at[pl.ds(pl.multiple_of(c * 256 + x * 64 + zz * 8, 8), 8)],
                    landing.at[k],
                    device,
                )
                for k, (zz, device) in enumerate(along_z)
            ],
            landing,
        )

    def z_sum(buffer, landing, copies):
        arrived(copies)
        total = buffer[pl.ds(own, 8), :]
        for k in range(7):
            total = total + landing[k]
        return total

    def gather_z(full):
        piece = full.at[pl.ds(own, 8)]
        return group([(piece, piece, device) for _, device in along_z], full.at[pl.ds(0, 56)])

    def gather_x(full, copies):
        arrived(copies)
        piece = full.at[pl.ds(block, 64)]
        return group([(piece, piece, device) for _, device in along_x], full.at[pl.ds(0, 192)])

    def gather_core(full, copies):
        arrived(copies)
        piece = full.at[pl.ds(half, 256)]
        return group([(piece, piece, core)], piece)

    def exchange_y(slots, mine, count):
        piece = slots.at[mine]
        return group([(piece, piece, along_y[k]) for k in range(count)], slots.at[pl.ds(0, count)])

    rows = pl.ds(own, 8)
    half_rows = pl.ds(half, 256)
    gram_half = pl.ds(pl.multiple_of(c * 128, 128), 128)
    gram_rows = pl.ds(pl.multiple_of(c * 128 + z * 16, 16), 16)

    loads["w2"].wait()
    loads["v1"].wait()
    w2_t, v1 = split(w2_ref[...].T), split(v1_ref[...])
    gram[...] = dot(w2_t, v1)
    loads["cap2"].wait()
    cap2_all[rows, :] = jnp.concatenate([cap2_ref[:, 0:256], cap2_ref[:, 256:512]], axis=0)
    loads["cap0"].wait()
    cap0_y[y % 2] = cap0_ref[...]

    pl.semaphore_wait(barrier, len(everyone))
    gram_copies = group(
        [(gram.at[pl.ds(pl.multiple_of(other * 128, 128), 128)], gram_c, core)], gram_c
    )
    cap2_copies = gather_z(cap2_all)
    cap0_copies = group([(cap0_ref, cap0_y.at[y % 2], along_y[0])], cap0_ref)

    loads["v0"].wait()
    loads["w1"].wait()
    v0 = split(v0_ref[...])
    cross[0:256, :] = dot(w2_t, v0)
    cross[256:512, :] = dot(split(w1_ref[...].T), v0)
    cross_copies = core_step(cross, cross_c)

    arrived(gram_copies)
    gram[gram_half, :] += gram_c[...]
    gram_copies = group(
        [
            (gram.at[pl.ds(pl.multiple_of(c * 128 + zz * 16, 16), 16)], gram_z.at[k], device)
            for k, (zz, device) in enumerate(along_z)
        ],
        gram_z,
    )

    loads["x"].wait()
    loads["v2"].wait()
    x_t = split(x_ref[...].T)
    q2[...] = dot(x_t, split(v2_ref[...]))
    q2_copies = core_step(q2, q2_c)

    core_sum(cross, cross_c, cross_copies)
    cross_copies = x_step(cross, cross_x)

    q10[:, 0:256] = dot(x_t, v1)
    core_sum(q2, q2_c, q2_copies)
    q2_copies = x_step(q2, q2_x)
    q10[:, 256:512] = dot(x_t, v0)
    q10_copies = core_step(q10, q10_c)

    arrived(cap0_copies)
    loads["cap1"].wait()
    cap10_all[rows, 0:128] = jnp.concatenate(
        [cap1_ref[r : r + 1, 128 * q : 128 * q + 128] for r in range(2) for q in range(4)], axis=0
    )
    cap10_all[rows, 128:256] = jnp.concatenate(
        [cap0_y[r][:, 128 * q : 128 * q + 128] for r in range(2) for q in range(4)], axis=0
    )
    cap10_copies = gather_z(cap10_all)
    cap2_copies = gather_x(cap2_all, cap2_copies)

    arrived(gram_copies)
    total = gram[gram_rows, :]
    for k in range(7):
        total = total + gram_z[k]
    gram[gram_rows, :] = total
    gram_copies = group(
        [(gram.at[gram_rows], gram_x.at[k], device) for k, (_, device) in enumerate(along_x)],
        gram_x,
    )
    core_sum(q10, q10_c, q10_copies)
    x_sum(cross, cross_x, cross_copies)
    cross_copies = z_step(cross, cross_z)
    x_sum(q2, q2_x, q2_copies)
    q2_copies = z_step(q2, q2_z)
    q10_copies = x_step(q10, q10_x)

    arrived(gram_copies)
    gram_all[gram_rows, :] = total + (gram_x[0] + gram_x[1] + gram_x[2])
    piece = gram_all.at[gram_rows]
    gram_copies = group(
        [(piece, piece, device) for _, device in along_z], gram_all.at[pl.ds(0, 112)]
    )
    cap2_copies = gather_core(cap2_all, cap2_copies)
    cross_all[rows, :] = z_sum(cross, cross_z, cross_copies)
    cross_copies = gather_z(cross_all)
    q2_y[y % 2] = z_sum(q2, q2_z, q2_copies)
    q2_copies = exchange_y(q2_y, y % 2, 1)
    cap10_copies = gather_x(cap10_all, cap10_copies)

    arrived(cap2_copies)
    pieces = jnp.concatenate(split(cap2_all[...]), axis=1)
    halves = [
        pick(256, lambda i: slot_row(i // 4) + i % 4 + 4 * h, pieces) for h in range(2)
    ]
    cap2 = tuple(
        jnp.concatenate([h[:, k : k + 256] for h in halves], axis=1) for k in (0, 256)
    )
    x_sum(q10, q10_x, q10_copies)
    q10_copies = z_step(q10, q10_z)

    arrived(q2_copies)
    c2 = few_rows_dot(jnp.concatenate([q2_y[1], q2_y[0]], axis=1), cap2, ((1,), (1,)))
    c2_all[rows, :] = c2
    c2_copies = gather_z(c2_all)
    arrived(gram_copies)
    piece = gram_all.at[gram_half]
    gram_copies = group([(piece, piece, core)], piece)
    cross_copies = gather_x(cross_all, cross_copies)
    arrived(cap10_copies)
    cap10_copies = group(
        [
            (cap10_all.at[half_rows, 0:128], cap10_y.at[half_rows, 0:128], along_y[0]),
            (cap10_all.at[half_rows, 128:256], cap10_y.at[half_rows, 128:256], along_y[1]),
        ],
        cap10_y.at[half_rows],
    )
    arrived(gram_copies)
    step = few_rows_dot(c2, split(gram_all[...]))
    q10_own = z_sum(q10, q10_z, q10_copies)
    q1_y[y % 4] = q10_own[:, 0:256] - step
    q1_copies = exchange_y(q1_y, y % 4, 3)

    c2_copies = gather_x(c2_all, c2_copies)
    arrived(cap10_copies)
    cap10_copies = group(
        [(b.at[half_rows], b.at[half_rows], core) for b in (cap10_all, cap10_y)], cap10_all
    )
    cross_copies = gather_core(cross_all, cross_copies)
    arrived(cap10_copies)
    even, even_pair = y % 2 == 0, (y // 2) % 2 == 0
    mine, theirs = cap10_all[:, 0:128], cap10_y[:, 0:128]
    cap1 = paired_rows(
        lambda i: slot_row(i // 2) + 4 * (i % 2),
        jnp.where(even, mine, theirs),
        jnp.where(even, theirs, mine),
    )

    arrived(q1_copies)
    c1 = few_rows_dot(
        jnp.concatenate([q1_y[2] + q1_y[3], q1_y[0] + q1_y[1]], axis=1), cap1, ((1,), (1,))
    )
    c1_all[rows, :] = c1
    arrived(cross_copies)
    q0_y[y] = q10_own[:, 256:512] - few_rows_dot(
        jnp.concatenate([c2, c1], axis=1), split(cross_all[...])
    )
    q0_copies = exchange_y(q0_y, y, 7)
    c1_copies = gather_z(c1_all)
    mine, theirs = cap10_all[:, 128:256], cap10_y[:, 128:256]
    cap0 = paired_rows(
        lambda i: slot_row(i % 64) + 4 * (i // 64),
        jnp.where(even_pair, mine, theirs),
        jnp.where(even_pair, theirs, mine),
    )
    c2_copies = gather_core(c2_all, c2_copies)

    arrived(q0_copies)
    c0 = few_rows_dot(
        jnp.concatenate(
            [(q0_y[4] + q0_y[5]) + (q0_y[6] + q0_y[7]), (q0_y[0] + q0_y[1]) + (q0_y[2] + q0_y[3])],
            axis=1,
        ),
        cap0,
        ((1,), (1,)),
    )
    c0_all[rows, :] = c0
    c0_copies = gather_z(c0_all)
    c1_copies = gather_x(c1_all, c1_copies)
    arrived(c2_copies)
    out_ref[...] = x_ref[...] - dot(split(w2_ref[...]), split(c2_all[...]), ((1,), (1,)))
    c0_copies = gather_x(c0_all, c0_copies)
    c1_copies = gather_core(c1_all, c1_copies)
    arrived(c1_copies)
    out_ref[...] -= dot(split(w1_ref[...]), split(c1_all[...]), ((1,), (1,)))
    loads["w0"].wait()
    w0 = split(w0_ref[...])
    left()
    c0_copies = gather_core(c0_all, c0_copies)
    out_ref[:, half_rows] -= dot(w0, split(c0_all[half_rows, :]), ((1,), (1,)))
    arrived(c0_copies)
    half_rows = pl.ds(other_half, 256)
    out_ref[:, half_rows] -= dot(w0, split(c0_all[half_rows, :]), ((1,), (1,)))
    left()


def shards(
    rhs, v_basis0, w_basis0, cap_inv0, v_basis1, w_basis1, cap_inv1, v_basis2, w_basis2, cap_inv2
):
    groups = 37

    def f32(*shape):
        return pltpu.VMEM(shape, F32)

    return pl.pallas_call(
        kernel,
        out_shape=jax.ShapeDtypeStruct(rhs.shape, F32),
        in_specs=[pl.BlockSpec(memory_space=pltpu.HBM)] * 10,
        out_specs=pl.BlockSpec(memory_space=pltpu.VMEM),
        scratch_shapes=[
            f32(256, 512), f32(256, 256), f32(256, 256), f32(1, 512), f32(256, 256),
            f32(256, 256), f32(2, 512), f32(256, 256), f32(256, 256), f32(4, 512),
            pltpu.SemaphoreType.DMA((10,)),
            f32(256, 256), f32(128, 256), f32(7, 16, 256), f32(3, 16, 256), f32(256, 256),
            f32(512, 256), f32(512, 256), f32(512, 512),
            f32(256, 256), f32(256, 256), f32(256, 512),
            f32(3, 64, 256), f32(3, 64, 256), f32(3, 64, 512),
            f32(7, 8, 256), f32(7, 8, 256), f32(7, 8, 512),
            f32(512, 256), f32(512, 256), f32(512, 256), f32(512, 256),
            f32(512, 256), f32(512, 256), f32(512, 256),
            f32(2, 1, 512), f32(2, 8, 256), f32(4, 8, 256), f32(8, 8, 256),
            pltpu.SemaphoreType.DMA((groups,)),
            pltpu.SemaphoreType.DMA((groups,)),
        ],
        compiler_params=pltpu.CompilerParams(
            collective_id=0, has_side_effects=True, vmem_limit_bytes=52000 * 1024
        ),
    )(
        *(
            pltpu.with_memory_space_constraint(argument, pltpu.HBM)
            for argument in (
                rhs, v_basis0, w_basis0, cap_inv0, v_basis1, w_basis1, cap_inv1,
                v_basis2, w_basis2, cap_inv2,
            )
        )
    )


def solution(mesh):
    rows = P("rows", None)
    return jax.shard_map(
        shards, mesh=mesh, in_specs=(rows,) * 10, out_specs=rows, check_vma=False
    )
```

time: 86.7 us -> 65.5 us (0.76)
  Pallas kernels: 76.7 us -> 64.6 us
  local copies, waits for them, and re-layouts: 9.6 us -> 0.8 us
    pallas_call x1, Pallas kernels: 76.7 us -> 64.6 us  [shards(): pl.pallas_call(kernel, out_shape=jax.ShapeDtypeStruct(rhs.shape, F32), in...]
    unnamed x21 -> x1, local copies, waits for them, and re-layouts: 9.6 us -> 0.8 us
where the time goes in v2:
time: 65.5 us; the launch traced here: 65.4 us
  Pallas kernels  64.6 us (99%)
  local copies, waits for them, and re-layouts  0.8 us (1%)
    pallas_call x1, Pallas kernels, shards(): pl.pallas_call(kernel, out_shape=jax.ShapeDtypeStruct(rhs.shape, F32), in...  64.6 us

profile of v2, /device:TPU:1, one launch (start us, length us, event | category | flops | bytes accessed | tf_op | source)
XLA Modules:
  0.0 65.4 jit_solution(15005128986480317617)
XLA Ops:
  0.0 64.6 %shard_map.100 = f32[256,512]{1,0:T(8,128)S(1)} custom-call(f32[256,512]{1,0:T(8,128)} %x_hbm.1, f32[256,256]{1,0:T(8,128)} %v0_hbm.1, f32[256,256]{1,0:T(8,128)} %w0_hbm.1, f32[1,512]{1,0:T(1,128)} %cap0_hbm.1, f32[256,256]{1,0:T(8,128)} %v1_hbm.1, f32[256,256]{1,0:T(8,128)} %w1_hbm.1, f32[2,512]{1,0:T(2,128)} %cap1_hbm.1, f32[256,256]{1,0:T(8,128)} %v2_hbm.1, ...), custom_call_target="tpu_custom_call" | custom-call | tf_op jit(solution)/shard_map/pallas_call | solution.py:393
  64.6 0.8 %copy.12 = f32[256,512]{1,0:T(8,128)} copy(f32[256,512]{1,0:T(8,128)S(1)} %shard_map.100) | data formatting | bytes 1048576

commit v3 on v2

--- a/solution.py
+++ b/solution.py
@@ -1,3 +1,5 @@
+import math
+
 import jax
 import jax.numpy as jnp
 from jax import lax
@@ -59,10 +61,11 @@
     out_ref,
     x_ref, v0_ref, w0_ref, cap0_ref, v1_ref, w1_ref, cap1_ref, v2_ref, w2_ref, cap2_ref, load_sem,
     gram, gram_c, gram_z, gram_x, gram_all,
-    q2, cross, q10, q2_c, cross_c, q10_c, q2_x, cross_x, q10_x, q2_z, cross_z, q10_z,
+    q2, cross, q1, q0, q2_c, cross_c, q1_c, q0_c, q2_x, cross_x, q1_x, q0_x,
+    q2_z, cross_z, q1_z, q0_z,
     cross_all, cap2_all, cap10_all, cap10_y, c2_all, c1_all, c0_all,
     cap0_y, q2_y, q1_y, q0_y,
-    send_sem, recv_sem,
+    all_sent, send_sem, recv_sem,
 ):
     me = lax.axis_index("rows")
     y, x, z, c = me // 64, (me // 16) % 4, (me // 2) % 8, me % 2
@@ -83,21 +86,21 @@
         return b2 * 4 + b1 * 2 + b0
 
     core = at(y, x, z, other)
-    along_x = [((x + k) % 4, at(y, (x + k) % 4, z, c)) for k in range(1, 4)]
-    along_z = [((z + k) % 8, at(y, x, (z + k) % 8, c)) for k in range(1, 8)]
-    along_y = [at(flip(k), x, z, c) for k in range(1, 8)]
+    along_x = [((x + k) % 4, at(y, (x + k) % 4, z, c)) for k in (2, 1, 3)]
+    along_z = [((z + k) % 8, at(y, x, (z + k) % 8, c)) for k in (4, 3, 5, 2, 6, 1, 7)]
+    along_y = {k: at(flip(k), x, z, c) for k in (4, 5, 3, 6, 2, 7, 1)}
 
     barrier = pltpu.get_barrier_semaphore()
-    everyone = [core] + [d for _, d in along_x] + [d for _, d in along_z] + along_y
+    everyone = [core] + [d for _, d in along_x] + [d for _, d in along_z] + list(along_y.values())
     for device in everyone:
         pl.semaphore_signal(barrier, inc=1, device_id=(device,), device_id_type=MESH)
 
     loads = {}
     for index, (name, source, target) in enumerate(
         [
-            ("w2", w2_hbm, w2_ref), ("v1", v1_hbm, v1_ref), ("cap2", cap2_hbm, cap2_ref),
-            ("cap0", cap0_hbm, cap0_ref), ("cap1", cap1_hbm, cap1_ref), ("x", x_hbm, x_ref),
-            ("v2", v2_hbm, v2_ref), ("v0", v0_hbm, v0_ref), ("w1", w1_hbm, w1_ref),
+            ("w2", w2_hbm, w2_ref), ("v0", v0_hbm, v0_ref), ("w1", w1_hbm, w1_ref),
+            ("cap0", cap0_hbm, cap0_ref), ("cap2", cap2_hbm, cap2_ref), ("v1", v1_hbm, v1_ref),
+            ("x", x_hbm, x_ref), ("v2", v2_hbm, v2_ref), ("cap1", cap1_hbm, cap1_ref),
             ("w0", w0_hbm, w0_ref),
         ]
     ):
@@ -105,21 +108,27 @@
         loads[name].start()
 
     used = [0]
-    sent = []
+    sent = [0]
 
     def group(moves, size_like):
         index = used[0]
         used[0] += 1
+        size = math.prod(size_like.shape) // K
+        bucket = len(sent) - 1 if size >= 8 else send_sem.shape[0] - 1
+        if size >= 8 and sent[-1] + size > all_sent.shape[0]:
+            bucket = len(sent)
+            sent.append(0)
+        if size >= 8:
+            sent[bucket] += size
         for source, target, device in moves:
             pltpu.make_async_remote_copy(
                 src_ref=source,
                 dst_ref=target,
-                send_sem=send_sem.at[index],
+                send_sem=send_sem.at[bucket],
                 recv_sem=recv_sem.at[index],
                 device_id=(device,),
                 device_id_type=MESH,
             ).start()
-        sent.append((index, size_like))
         return index, size_like
 
     def arrived(one_group):
@@ -127,9 +136,10 @@
         pltpu.make_async_copy(size_like, size_like, recv_sem.at[index]).wait()
 
     def left():
-        for index, size_like in sent:
-            pltpu.make_async_copy(size_like, size_like, send_sem.at[index]).wait()
-        sent.clear()
+        for index, size in enumerate(sent):
+            amount = all_sent.at[pl.ds(0, size)]
+            pltpu.make_async_copy(amount, amount, send_sem.at[index]).wait()
+        pltpu.make_async_copy(cap0_ref, cap0_ref, send_sem.at[send_sem.shape[0] - 1]).wait()
 
     def core_step(buffer, landing):
         return group([(buffer.at[pl.ds(other_half, 256)], landing, core)], landing)
@@ -191,7 +201,8 @@
 
     def exchange_y(slots, mine, count):
         piece = slots.at[mine]
-        return group([(piece, piece, along_y[k]) for k in range(count)], slots.at[pl.ds(0, count)])
+        devices = [device for k, device in along_y.items() if k <= count]
+        return group([(piece, piece, device) for device in devices], slots.at[pl.ds(0, count)])
 
     rows = pl.ds(own, 8)
     half_rows = pl.ds(half, 256)
@@ -199,27 +210,35 @@
     gram_rows = pl.ds(pl.multiple_of(c * 128 + z * 16, 16), 16)
 
     loads["w2"].wait()
-    loads["v1"].wait()
-    w2_t, v1 = split(w2_ref[...].T), split(v1_ref[...])
-    gram[...] = dot(w2_t, v1)
+    loads["v0"].wait()
+    w2_t, v0 = split(w2_ref[...].T), split(v0_ref[...])
+    cross[0:256, :] = dot(w2_t, v0)
+    loads["w1"].wait()
+    cross[256:512, :] = dot(split(w1_ref[...].T), v0)
+    loads["cap0"].wait()
+    cap0_y[y % 2] = cap0_ref[...]
     loads["cap2"].wait()
     cap2_all[rows, :] = jnp.concatenate([cap2_ref[:, 0:256], cap2_ref[:, 256:512]], axis=0)
-    loads["cap0"].wait()
-    cap0_y[y % 2] = cap0_ref[...]
 
     pl.semaphore_wait(barrier, len(everyone))
+    cross_copies = core_step(cross, cross_c)
+    cap0_copies = group([(cap0_ref, cap0_y.at[y % 2], along_y[1])], cap0_ref)
+    cap2_copies = gather_z(cap2_all)
+
+    loads["v1"].wait()
+    v1 = split(v1_ref[...])
+    gram[...] = dot(w2_t, v1)
     gram_copies = group(
         [(gram.at[pl.ds(pl.multiple_of(other * 128, 128), 128)], gram_c, core)], gram_c
     )
-    cap2_copies = gather_z(cap2_all)
-    cap0_copies = group([(cap0_ref, cap0_y.at[y % 2], along_y[0])], cap0_ref)
-
-    loads["v0"].wait()
-    loads["w1"].wait()
-    v0 = split(v0_ref[...])
-    cross[0:256, :] = dot(w2_t, v0)
-    cross[256:512, :] = dot(split(w1_ref[...].T), v0)
-    cross_copies = core_step(cross, cross_c)
+    core_sum(cross, cross_c, cross_copies)
+    cross_copies = x_step(cross, cross_x)
+
+    loads["x"].wait()
+    loads["v2"].wait()
+    x_t = split(x_ref[...].T)
+    q2[...] = dot(x_t, split(v2_ref[...]))
+    q2_copies = core_step(q2, q2_c)
 
     arrived(gram_copies)
     gram[gram_half, :] += gram_c[...]
@@ -231,21 +250,6 @@
         gram_z,
     )
 
-    loads["x"].wait()
-    loads["v2"].wait()
-    x_t = split(x_ref[...].T)
-    q2[...] = dot(x_t, split(v2_ref[...]))
-    q2_copies = core_step(q2, q2_c)
-
-    core_sum(cross, cross_c, cross_copies)
-    cross_copies = x_step(cross, cross_x)
-
-    q10[:, 0:256] = dot(x_t, v1)
-    core_sum(q2, q2_c, q2_copies)
-    q2_copies = x_step(q2, q2_x)
-    q10[:, 256:512] = dot(x_t, v0)
-    q10_copies = core_step(q10, q10_c)
-
     arrived(cap0_copies)
     loads["cap1"].wait()
     cap10_all[rows, 0:128] = jnp.concatenate(
@@ -255,7 +259,16 @@
         [cap0_y[r][:, 128 * q : 128 * q + 128] for r in range(2) for q in range(4)], axis=0
     )
     cap10_copies = gather_z(cap10_all)
+
+    core_sum(q2, q2_c, q2_copies)
+    q2_copies = x_step(q2, q2_x)
+    q1[...] = dot(x_t, v1)
+    q1_copies = core_step(q1, q1_c)
     cap2_copies = gather_x(cap2_all, cap2_copies)
+    x_sum(cross, cross_x, cross_copies)
+    cross_copies = z_step(cross, cross_z)
+    q0[...] = dot(x_t, v0)
+    q0_copies = core_step(q0, q0_c)
 
     arrived(gram_copies)
     total = gram[gram_rows, :]
@@ -266,25 +279,35 @@
         [(gram.at[gram_rows], gram_x.at[k], device) for k, (_, device) in enumerate(along_x)],
         gram_x,
     )
-    core_sum(q10, q10_c, q10_copies)
-    x_sum(cross, cross_x, cross_copies)
-    cross_copies = z_step(cross, cross_z)
+    cap10_copies = gather_x(cap10_all, cap10_copies)
     x_sum(q2, q2_x, q2_copies)
     q2_copies = z_step(q2, q2_z)
-    q10_copies = x_step(q10, q10_x)
-
+    core_sum(q1, q1_c, q1_copies)
+    q1_copies = x_step(q1, q1_x)
+    core_sum(q0, q0_c, q0_copies)
+
+    cross_all[rows, :] = z_sum(cross, cross_z, cross_copies)
+    cross_copies = gather_z(cross_all)
     arrived(gram_copies)
     gram_all[gram_rows, :] = total + (gram_x[0] + gram_x[1] + gram_x[2])
     piece = gram_all.at[gram_rows]
     gram_copies = group(
         [(piece, piece, device) for _, device in along_z], gram_all.at[pl.ds(0, 112)]
     )
+    q0_copies = x_step(q0, q0_x)
     cap2_copies = gather_core(cap2_all, cap2_copies)
-    cross_all[rows, :] = z_sum(cross, cross_z, cross_copies)
-    cross_copies = gather_z(cross_all)
     q2_y[y % 2] = z_sum(q2, q2_z, q2_copies)
     q2_copies = exchange_y(q2_y, y % 2, 1)
-    cap10_copies = gather_x(cap10_all, cap10_copies)
+    arrived(cap10_copies)
+    cap10_copies = group(
+        [
+            (cap10_all.at[half_rows, 0:128], cap10_y.at[half_rows, 0:128], along_y[1]),
+            (cap10_all.at[half_rows, 128:256], cap10_y.at[half_rows, 128:256], along_y[2]),
+        ],
+        cap10_y.at[half_rows],
+    )
+    x_sum(q1, q1_x, q1_copies)
+    q1_copies = z_step(q1, q1_z)
 
     arrived(cap2_copies)
     pieces = jnp.concatenate(split(cap2_all[...]), axis=1)
@@ -294,37 +317,26 @@
     cap2 = tuple(
         jnp.concatenate([h[:, k : k + 256] for h in halves], axis=1) for k in (0, 256)
     )
-    x_sum(q10, q10_x, q10_copies)
-    q10_copies = z_step(q10, q10_z)
-
+    cross_copies = gather_x(cross_all, cross_copies)
     arrived(q2_copies)
     c2 = few_rows_dot(jnp.concatenate([q2_y[1], q2_y[0]], axis=1), cap2, ((1,), (1,)))
     c2_all[rows, :] = c2
-    c2_copies = gather_z(c2_all)
     arrived(gram_copies)
     piece = gram_all.at[gram_half]
     gram_copies = group([(piece, piece, core)], piece)
-    cross_copies = gather_x(cross_all, cross_copies)
-    arrived(cap10_copies)
-    cap10_copies = group(
-        [
-            (cap10_all.at[half_rows, 0:128], cap10_y.at[half_rows, 0:128], along_y[0]),
-            (cap10_all.at[half_rows, 128:256], cap10_y.at[half_rows, 128:256], along_y[1]),
-        ],
-        cap10_y.at[half_rows],
-    )
-    arrived(gram_copies)
-    step = few_rows_dot(c2, split(gram_all[...]))
-    q10_own = z_sum(q10, q10_z, q10_copies)
-    q1_y[y % 4] = q10_own[:, 0:256] - step
-    q1_copies = exchange_y(q1_y, y % 4, 3)
-
-    c2_copies = gather_x(c2_all, c2_copies)
     arrived(cap10_copies)
     cap10_copies = group(
         [(b.at[half_rows], b.at[half_rows], core) for b in (cap10_all, cap10_y)], cap10_all
     )
+    x_sum(q0, q0_x, q0_copies)
+    q0_copies = z_step(q0, q0_z)
+    q1_own = z_sum(q1, q1_z, q1_copies)
+    arrived(gram_copies)
+    q1_y[y % 4] = q1_own - few_rows_dot(c2, split(gram_all[...]))
+    q1_copies = exchange_y(q1_y, y % 4, 3)
+    c2_copies = gather_z(c2_all)
     cross_copies = gather_core(cross_all, cross_copies)
+
     arrived(cap10_copies)
     even, even_pair = y % 2 == 0, (y // 2) % 2 == 0
     mine, theirs = cap10_all[:, 0:128], cap10_y[:, 0:128]
@@ -333,18 +345,20 @@
         jnp.where(even, mine, theirs),
         jnp.where(even, theirs, mine),
     )
+    arrived(cross_copies)
+    cross_high, cross_low = split(cross_all[...])
+    q0_own = z_sum(q0, q0_z, q0_copies)
+    q0_own = q0_own - few_rows_dot(c2, (cross_high[0:256], cross_low[0:256]))
 
     arrived(q1_copies)
     c1 = few_rows_dot(
         jnp.concatenate([q1_y[2] + q1_y[3], q1_y[0] + q1_y[1]], axis=1), cap1, ((1,), (1,))
     )
     c1_all[rows, :] = c1
-    arrived(cross_copies)
-    q0_y[y] = q10_own[:, 256:512] - few_rows_dot(
-        jnp.concatenate([c2, c1], axis=1), split(cross_all[...])
-    )
+    q0_y[y] = q0_own - few_rows_dot(c1, (cross_high[256:512], cross_low[256:512]))
     q0_copies = exchange_y(q0_y, y, 7)
     c1_copies = gather_z(c1_all)
+    c2_copies = gather_x(c2_all, c2_copies)
     mine, theirs = cap10_all[:, 128:256], cap10_y[:, 128:256]
     cap0 = paired_rows(
         lambda i: slot_row(i % 64) + 4 * (i // 64),
@@ -373,7 +387,6 @@
     out_ref[...] -= dot(split(w1_ref[...]), split(c1_all[...]), ((1,), (1,)))
     loads["w0"].wait()
     w0 = split(w0_ref[...])
-    left()
     c0_copies = gather_core(c0_all, c0_copies)
     out_ref[:, half_rows] -= dot(w0, split(c0_all[half_rows, :]), ((1,), (1,)))
     arrived(c0_copies)
@@ -385,7 +398,7 @@
 def shards(
     rhs, v_basis0, w_basis0, cap_inv0, v_basis1, w_basis1, cap_inv1, v_basis2, w_basis2, cap_inv2
 ):
-    groups = 37
+    groups = 40
 
     def f32(*shape):
         return pltpu.VMEM(shape, F32)
@@ -400,14 +413,12 @@
             f32(256, 256), f32(2, 512), f32(256, 256), f32(256, 256), f32(4, 512),
             pltpu.SemaphoreType.DMA((10,)),
             f32(256, 256), f32(128, 256), f32(7, 16, 256), f32(3, 16, 256), f32(256, 256),
-            f32(512, 256), f32(512, 256), f32(512, 512),
-            f32(256, 256), f32(256, 256), f32(256, 512),
-            f32(3, 64, 256), f32(3, 64, 256), f32(3, 64, 512),
-            f32(7, 8, 256), f32(7, 8, 256), f32(7, 8, 512),
+            *[f32(512, 256)] * 4, *[f32(256, 256)] * 4, *[f32(3, 64, 256)] * 4, *[f32(7, 8, 256)] * 4,
             f32(512, 256), f32(512, 256), f32(512, 256), f32(512, 256),
             f32(512, 256), f32(512, 256), f32(512, 256),
             f32(2, 1, 512), f32(2, 8, 256), f32(4, 8, 256), f32(8, 8, 256),
-            pltpu.SemaphoreType.DMA((groups,)),
+            f32(1024, 256),
+            pltpu.SemaphoreType.DMA((9,)),
             pltpu.SemaphoreType.DMA((groups,)),
         ],
         compiler_params=pltpu.CompilerParams(

time: 65.5 us -> 61 us (0.931)
  Pallas kernels: 64.6 us -> 60 us
    pallas_call x1, Pallas kernels: 64.6 us -> 60 us  [shards(): pl.pallas_call(kernel, out_shape=jax.ShapeDtypeStruct(rhs.shape, F32), in...]
where the time goes in v3:
time: 61 us; the launch traced here: 60.8 us
  Pallas kernels  60 us (98%)
  local copies, waits for them, and re-layouts  0.8 us (1%)
    pallas_call x1, Pallas kernels, shards(): pl.pallas_call(kernel, out_shape=jax.ShapeDtypeStruct(rhs.shape, F32), in...  60 us

profile of v3, /device:TPU:1, one launch (start us, length us, event | category | flops | bytes accessed | tf_op | source)
XLA Modules:
  0.0 60.8 jit_solution(5515411373635396285)
XLA Ops:
  0.0 60.0 %shard_map.100 = f32[256,512]{1,0:T(8,128)S(1)} custom-call(f32[256,512]{1,0:T(8,128)} %x_hbm.1, f32[256,256]{1,0:T(8,128)} %v0_hbm.1, f32[256,256]{1,0:T(8,128)} %w0_hbm.1, f32[1,512]{1,0:T(1,128)} %cap0_hbm.1, f32[256,256]{1,0:T(8,128)} %v1_hbm.1, f32[256,256]{1,0:T(8,128)} %w1_hbm.1, f32[2,512]{1,0:T(2,128)} %cap1_hbm.1, f32[256,256]{1,0:T(8,128)} %v2_hbm.1, ...), custom_call_target="tpu_custom_call" | custom-call | tf_op jit(solution)/shard_map/pallas_call | solution.py:406
  60.0 0.8 %copy.12 = f32[256,512]{1,0:T(8,128)} copy(f32[256,512]{1,0:T(8,128)S(1)} %shard_map.100) | data formatting | bytes 1048576

commit v4 on v3

--- a/solution.py
+++ b/solution.py
@@ -285,6 +285,7 @@
     core_sum(q1, q1_c, q1_copies)
     q1_copies = x_step(q1, q1_x)
     core_sum(q0, q0_c, q0_copies)
+    q0_copies = x_step(q0, q0_x)
 
     cross_all[rows, :] = z_sum(cross, cross_z, cross_copies)
     cross_copies = gather_z(cross_all)
@@ -294,7 +295,6 @@
     gram_copies = group(
         [(piece, piece, device) for _, device in along_z], gram_all.at[pl.ds(0, 112)]
     )
-    q0_copies = x_step(q0, q0_x)
     cap2_copies = gather_core(cap2_all, cap2_copies)
     q2_y[y % 2] = z_sum(q2, q2_z, q2_copies)
     q2_copies = exchange_y(q2_y, y % 2, 1)
@@ -318,6 +318,8 @@
         jnp.concatenate([h[:, k : k + 256] for h in halves], axis=1) for k in (0, 256)
     )
     cross_copies = gather_x(cross_all, cross_copies)
+    x_sum(q0, q0_x, q0_copies)
+    q0_copies = z_step(q0, q0_z)
     arrived(q2_copies)
     c2 = few_rows_dot(jnp.concatenate([q2_y[1], q2_y[0]], axis=1), cap2, ((1,), (1,)))
     c2_all[rows, :] = c2
@@ -328,8 +330,6 @@
     cap10_copies = group(
         [(b.at[half_rows], b.at[half_rows], core) for b in (cap10_all, cap10_y)], cap10_all
     )
-    x_sum(q0, q0_x, q0_copies)
-    q0_copies = z_step(q0, q0_z)
     q1_own = z_sum(q1, q1_z, q1_copies)
     arrived(gram_copies)
     q1_y[y % 4] = q1_own - few_rows_dot(c2, split(gram_all[...]))

time: 61 us -> 60.9 us (level)
  no operation moved by 1% of the time
where the time goes in v4:
time: 60.9 us; the launch traced here: 60.8 us
  Pallas kernels  59.9 us (98%)
  local copies, waits for them, and re-layouts  0.8 us (1%)
    pallas_call x1, Pallas kernels, shards(): pl.pallas_call(kernel, out_shape=jax.ShapeDtypeStruct(rhs.shape, F32), in...  59.9 us

profile of v4, /device:TPU:1, one launch (start us, length us, event | category | flops | bytes accessed | tf_op | source)
XLA Modules:
  0.0 60.8 jit_solution(16227517207317444899)
XLA Ops:
  0.0 59.9 %shard_map.100 = f32[256,512]{1,0:T(8,128)S(1)} custom-call(f32[256,512]{1,0:T(8,128)} %x_hbm.1, f32[256,256]{1,0:T(8,128)} %v0_hbm.1, f32[256,256]{1,0:T(8,128)} %w0_hbm.1, f32[1,512]{1,0:T(1,128)} %cap0_hbm.1, f32[256,256]{1,0:T(8,128)} %v1_hbm.1, f32[256,256]{1,0:T(8,128)} %w1_hbm.1, f32[2,512]{1,0:T(2,128)} %cap1_hbm.1, f32[256,256]{1,0:T(8,128)} %v2_hbm.1, ...), custom_call_target="tpu_custom_call" | custom-call | tf_op jit(solution)/shard_map/pallas_call | solution.py:406
  60.0 0.8 %copy.12 = f32[256,512]{1,0:T(8,128)} copy(f32[256,512]{1,0:T(8,128)S(1)} %shard_map.100) | data formatting | bytes 1048576
